TPU v7x, 32 devices: a whole 2x2x4 slice. The times are simulated.
32 devices in a mesh: video: 2 (over y), rows: 4 (over z), cols: 4 (over x, core).
Axes of the slice: x: 2, y: 2, z: 4, core: 2. Of those that a mesh axis runs over, the one named last changes fastest.
Arguments:
- frame_in: bfloat16 [64, 80, 512], P(('video', 'rows'), 'cols'), parts along dimension 0, may hold values from -6 to 6
- norm_gain: float32 [512], replicated, may hold values from 0.5 to 1.5
- w_query: bfloat16 [512, 512], replicated, may hold values from -2 to 2
- w_key: bfloat16 [512, 512], replicated, may hold values from -0.125 to 0.125
- w_value: bfloat16 [512, 512], replicated, may hold values from -0.25 to 0.25
- w_out: bfloat16 [512, 512], replicated, may hold values from -0.25 to 0.25
- conv_gain: float32 [512], replicated, may hold values from 0.5 to 1.5
- conv_cache: bfloat16 [2, 64, 80, 512], P(None, ('video', 'rows'), 'cols'), parts along dimension 1, may hold values from -6 to 6
- w_conv: bfloat16 [3, 3, 3, 512, 256], replicated, may hold values from -0.0546875 to 0.0546875
- conv_bias: float32 [256], replicated, may hold values from -0.5 to 0.5
Outputs:
- hidden: bfloat16 [64, 80, 512], P(('video', 'rows'), 'cols'), parts along dimension 0
- mixed_out: bfloat16 [64, 80, 256], P(('video', 'rows'), 'cols'), parts along dimension 0
There are 2 independent parts, one for each index of `video`. A program takes and returns all parts, laid end to end along the dimension named above; an argument that names none is the same for every part. Nothing has to cross between parts.
All inputs are finite; a program needn't handle non-finite values.
Results may differ from a plain program's by a relative error of at most 0.012.
Values may be sent and summed in bfloat16 or wider, within the bound.
No kernel may reach another device: no remote copies, remote signals or barrier semaphores. Data moves between devices by JAX's collectives and lax.ppermute only.
A program may use at most 128 MiB of HBM per device.

v0:
```python
import functools
import math

import jax
import jax.numpy as jnp
from jax import lax
from jax.experimental import pallas as pl
from jax.experimental.pallas import tpu as pltpu
from jax.sharding import PartitionSpec as P


EPS = 1e-06
AXES = ("rows", "cols")
F32 = jnp.float32
COST = 2_000_000_000
BF16 = jnp.bfloat16
VM = pl.BlockSpec(memory_space=pltpu.VMEM)


def near(value):
    return pltpu.with_memory_space_constraint(value, pltpu.VMEM)


def call(kernel, outs, args, limit=16 << 20, far_args=(), far=False, scratch=()):
    return pl.pallas_call(
        kernel,
        in_specs=[VM] * len(args) + [pl.BlockSpec(memory_space=pltpu.HBM)] * len(far_args),
        out_specs=[VM] * len(outs),
        out_shape=[
            jax.ShapeDtypeStruct(shape, dtype) if far else pltpu.VMEM(shape, dtype)
            for shape, dtype in outs
        ],
        scratch_shapes=scratch,
        compiler_params=pltpu.CompilerParams(vmem_limit_bytes=limit),
        cost_estimate=pl.CostEstimate(flops=COST, bytes_accessed=4 << 20, transcendentals=0),
    )(*[near(a) for a in args], *[pltpu.with_memory_space_constraint(a, pltpu.HBM) for a in far_args])


def chip_cycle(height, width):
    if width == 1 or height == 1:
        return [(z, x) for z in range(height) for x in range(width)]
    order = []
    for x in range(width):
        inner = range(1, height) if x % 2 == 0 else range(height - 1, 0, -1)
        order += [(z, x) for z in inner]
    return order + [(0, x) for x in range(width - 1, -1, -1)]


def permutations(rows, cols):
    def at(z, x, core):
        return z * cols + 2 * x + core

    walk = chip_cycle(rows, cols // 2)
    ring = []
    for k, here in enumerate(walk):
        there = walk[(k + 1) % len(walk)]
        ring += [(at(*here, 0), at(*there, 0)), (at(*there, 1), at(*here, 1))]
    twin = [(i, i ^ 1) for i in range(rows * cols)]
    down = [(i, i + cols) for i in range((rows - 1) * cols)]
    up = [(j, i) for i, j in down]
    cross = []
    for r in range(rows):
        for c in range(1, cols - 1, 2):
            i = r * cols + c
            cross += [(i, i + 1), (i + 1, i)]
    return len(walk), ring, twin, down, up, cross


def edge_slots(width):
    return -(-(width + 2) // 16) * 16


def edge_rows(width):
    return -(-width // 8) * 8


def side_slots(height):
    return height + 8


def rms_scaled(values, gain):
    mean_sq = jnp.mean(values * values, axis=-1, keepdims=True)
    return values * lax.rsqrt(mean_sq + EPS) * gain


def dot(a, b):
    return jnp.dot(a, b, preferred_element_type=F32)


def dot_t(a, b):
    return lax.dot_general(a, b, (((1,), (1,)), ((), ())), preferred_element_type=F32)


def row_edge(tile, r):
    width, _, channels = tile.shape
    fill = jnp.zeros((edge_rows(width) - width, channels), F32)
    return jnp.concatenate([tile[c, r : r + 1, :] for c in range(width)] + [fill], axis=0)


def load_tiles(frame_hbm, cache_hbm, gain_hbm, frame_ref, cache_ref, gain_ref, sems):
    copies = [
        pltpu.make_async_copy(frame_hbm, frame_ref, sems.at[0]),
        pltpu.make_async_copy(cache_hbm, cache_ref, sems.at[1]),
        pltpu.make_async_copy(gain_hbm, gain_ref, sems.at[2]),
    ]
    for copy in copies:
        copy.start()
    for copy in copies:
        copy.wait()


def pack_rows_kernel(frame_hbm, cache_hbm, gain_hbm, frame_ref, cache_ref, gain_ref, first_ref, last_ref, sems):
    load_tiles(frame_hbm, cache_hbm, gain_hbm, frame_ref, cache_ref, gain_ref, sems)
    height = frame_ref.shape[1]
    for t in range(3):
        tile = (frame_ref[...] if t == 2 else cache_ref[t]).astype(F32)
        first_ref[t] = row_edge(tile, 0).astype(BF16)
        last_ref[t] = row_edge(tile, height - 1).astype(BF16)


def faces_up():
    col = lax.axis_index("cols")
    return lax.rem(lax.rem(col, 2) + lax.div(col, 2), 2)


def pack_chain_kernel(frame_hbm, cache_hbm, gain_hbm, frame_ref, cache_ref, gain_ref, chain_ref, swap_ref, sems):
    load_tiles(frame_hbm, cache_hbm, gain_hbm, frame_ref, cache_ref, gain_ref, sems)
    width, height, channels = frame_ref.shape
    count, rows = width * height, edge_rows(width)
    up = faces_up()
    chain_ref[:count] = frame_ref[...].reshape(count, channels)
    swap_ref[:count] = frame_ref[...].reshape(count, channels)
    for t in range(2):
        tile = cache_ref[t].astype(F32)
        first, last = row_edge(tile, 0), row_edge(tile, height - 1)
        at = count + t * rows
        chain_ref[at : at + rows] = jnp.where(up == 1, first, last).astype(BF16)
        swap_ref[at : at + rows] = jnp.where(up == 1, last, first).astype(BF16)


def cut_kernel(arrived_ref, chain_ref):
    chain_ref[...] = arrived_ref[: chain_ref.shape[0]]


def split_kernel(cache_ref, a_ref, b_ref, edges_ref):
    _, width, height, _ = cache_ref.shape
    count, rows = width * height, edge_rows(width)
    up = faces_up()
    odd = lax.rem(lax.axis_index("cols"), 2)
    for k, ref in enumerate((a_ref, b_ref)):
        to = k * 3 * rows
        edges_ref[to : to + 2 * rows] = ref[count : count + 2 * rows]
        tile = ref[:count].astype(F32).reshape(width, height, -1)
        edge = jnp.where(up == 1, row_edge(tile, 0), row_edge(tile, height - 1))
        edges_ref[to + 2 * rows : to + 3 * rows] = edge.astype(BF16)
    for t in range(2):
        at = 6 * rows + t * height
        column = jnp.where(odd == 1, cache_ref[t, 0].astype(F32), cache_ref[t, width - 1].astype(F32))
        edges_ref[at : at + height] = column.astype(BF16)


def sort_edges_kernel(
    frame_ref, cache_ref, partner_ref, mine_ref, theirs_ref, top_ref, bottom_ref, twin_ref, cross_ref
):
    width, height, channels = frame_ref.shape
    count, rows = width * height, top_ref.shape[1]
    up = faces_up()
    odd = lax.rem(lax.axis_index("cols"), 2)
    row = lax.axis_index("rows")
    has_top, has_bottom = row > 0, row < lax.axis_size("rows") - 1
    fill = jnp.zeros((side_slots(height) - height - 2, channels), F32)
    for t in range(3):
        pair = []
        for k in range(2):
            mine = mine_ref[(3 * k + t) * rows : (3 * k + t + 1) * rows].astype(F32)
            theirs = theirs_ref[(3 - 3 * k + t) * rows : (4 - 3 * k + t) * rows].astype(F32)
            top = jnp.where(has_top, jnp.where(up == 1, theirs, mine), 0.0)
            bottom = jnp.where(has_bottom, jnp.where(up == 1, mine, theirs), 0.0)
            pair.append((top, bottom))
        (top, bottom), (twin_top, twin_bottom) = pair
        top_ref[t] = top.astype(BF16)
        bottom_ref[t] = bottom.astype(BF16)

        def facing(first, value, axis_rows):
            a, b = value[axis_rows(0)], value[axis_rows(width - 1)]
            return jnp.where(first, a, b)

        if t == 2:
            block = partner_ref[:count].astype(F32)
            column = facing(odd == 0, block, lambda c: slice(c * height, (c + 1) * height))
        else:
            at = 6 * rows + t * height
            column = theirs_ref[at : at + height].astype(F32)
        corners = [facing(odd == 0, v, lambda c: slice(c, c + 1)) for v in (twin_top, twin_bottom)]
        twin_ref[t] = jnp.concatenate([column, *corners, fill], axis=0).astype(BF16)
        tile = (frame_ref[...] if t == 2 else cache_ref[t]).astype(F32)
        column = jnp.where(odd == 0, tile[0], tile[width - 1])
        corners = [facing(odd == 0, v, lambda c: slice(c, c + 1)) for v in (top, bottom)]
        cross_ref[t] = jnp.concatenate([column, *corners, fill], axis=0).astype(BF16)


def pack_cols_kernel(frame_ref, cache_ref, top_ref, bottom_ref, twin_ref, cross_ref):
    width, height, channels = frame_ref.shape
    odd = lax.rem(lax.axis_index("cols"), 2)
    fill = jnp.zeros((side_slots(height) - height - 2, channels), F32)
    for t in range(3):
        sides = []
        for c in (0, width - 1):
            own = (frame_ref[c] if t == 2 else cache_ref[t, c]).astype(F32)
            top = top_ref[t].astype(F32)[c : c + 1, :]
            bottom = bottom_ref[t].astype(F32)[c : c + 1, :]
            sides.append(jnp.concatenate([own, top, bottom, fill], axis=0))
        left, right = sides
        twin_ref[t] = jnp.where(odd == 1, left, right).astype(BF16)
        cross_ref[t] = jnp.where(odd == 1, right, left).astype(BF16)


def extended(own, top, bottom, twin, cross, odd):
    height = twin.shape[0] - side_slots(0)
    left = jnp.where(odd == 1, twin, cross)
    right = jnp.where(odd == 1, cross, twin)
    width = own.shape[0] // height
    slots = edge_slots(width)
    slot = lax.broadcasted_iota(jnp.int32, (slots, own.shape[1]), 0)
    fill = jnp.zeros((slots - top.shape[0], own.shape[1]), F32)

    def edge(row, k):
        row = jnp.concatenate([row, fill], axis=0)
        row = jnp.where(slot == width, right[k : k + 1, :], row)
        return jnp.where(slot == slots - 1, left[k : k + 1, :], row)

    return jnp.concatenate(
        [edge(top, height), left[:height], own, right[:height], edge(bottom, height + 1)], axis=0
    )


def tap_rows(tokens, height, count):
    slots = edge_slots(count // height)
    main = tokens[slots : tokens.shape[0] - slots]
    mains = [main[j * height : j * height + count] for j in range(3)]
    result = []
    for edge in (tokens[:slots], None, tokens[tokens.shape[0] - slots :]):
        if edge is None:
            parts = mains
        else:
            edges = [pltpu.roll(edge, 1, 0), edge, pltpu.roll(edge, slots - 1, 0)]
            parts = [jnp.concatenate(pair, axis=0) for pair in zip(mains, edges)]
        result.append(jnp.concatenate([p.astype(BF16) for p in parts], axis=1))
    return result


def shifted_rows(sums, i, height, count):
    if i == 1:
        return sums
    main, edge = sums[:count], sums[count:]
    out = main.shape[1]
    width = count // height
    tile = main.reshape(width, height, out)
    moved = pltpu.roll(tile, 1 if i == 0 else height - 1, 1)
    row = lax.broadcasted_iota(jnp.int32, (height, out), 0)
    at = 0 if i == 0 else height - 1
    cells = [jnp.where(row == at, edge[c : c + 1, :], moved[c]) for c in range(width)]
    return jnp.concatenate(cells, axis=0)


def cache_conv_kernel(cache_ref, top_ref, bottom_ref, twin_ref, cross_ref, w_ref, out_ref):
    width, height, channels = cache_ref.shape[1:]
    count = width * height
    odd = lax.rem(lax.axis_index("cols"), 2)
    rows = [
        tap_rows(
            extended(
                cache_ref[t].reshape(count, channels).astype(F32),
                top_ref[t].astype(F32),
                bottom_ref[t].astype(F32),
                twin_ref[t].astype(F32),
                cross_ref[t].astype(F32),
                odd,
            ),
            height,
            count,
        )
        for t in range(2)
    ]
    result = None
    for i in range(3):
        patches = jnp.concatenate([rows[0][i], rows[1][i]], axis=1)
        taps = w_ref[:2, i].reshape(-1, w_ref.shape[4])
        value = shifted_rows(dot(patches, taps), i, height, count)
        result = value if result is None else result + value
    out_ref[...] = result


def query_kernel(
    frame_ref, top_ref, bottom_ref, twin_ref, cross_ref, gain_ref, wq_ref, wk_ref, raw_ref, keys_ref
):
    width, height, channels = frame_ref.shape
    odd = lax.rem(lax.axis_index("cols"), 2)
    tokens = extended(
        frame_ref[...].reshape(width * height, channels).astype(F32),
        top_ref[2].astype(F32),
        bottom_ref[2].astype(F32),
        twin_ref[2].astype(F32),
        cross_ref[2].astype(F32),
        odd,
    )
    raw_ref[...] = tokens.astype(BF16)
    normed = rms_scaled(tokens, gain_ref[...]).astype(BF16)
    rows = (dot(normed, wq_ref[...]) * (1.0 / math.sqrt(channels))).astype(BF16)
    keys_ref[...] = dot_t(rows, wk_ref[...]).astype(BF16)


def lanes(value, width):
    return jnp.broadcast_to(value, (value.shape[0], width))


def key_rows(refs, gain):
    parts = [
        rms_scaled(ref[...].reshape(-1, gain.shape[1]).astype(F32), gain).astype(BF16) for ref in refs
    ]
    return parts[0] if len(parts) == 1 else jnp.concatenate(parts, axis=0)


def fold_kernel(blocks, first, gain_ref, own_ref, twin_ref, *refs):
    keys = key_rows(refs[:blocks], gain_ref[...])
    states, outs = ((None, None), refs[blocks:]) if first else (refs[blocks:-2], refs[-2:])
    channels = keys.shape[1]
    length = own_ref.shape[0]
    all_scores = dot_t(jnp.concatenate([own_ref[...], twin_ref[...]], axis=0), keys)
    peaks, totals, weights = [], [], []
    for k, state in enumerate(states):
        scores = all_scores[k * length : (k + 1) * length]
        peak = jnp.max(scores, axis=1, keepdims=True)
        if not first:
            peak = jnp.maximum(peak, state[:, channels : channels + 1])
        part = jnp.exp(scores - peak)
        peaks.append(peak)
        totals.append(jnp.sum(part, axis=1, keepdims=True))
        weights.append(part.astype(BF16))
    all_summed = dot(jnp.concatenate(weights, axis=0), keys)
    for k, (state, out) in enumerate(zip(states, outs)):
        summed, total, peak = all_summed[k * length : (k + 1) * length], totals[k], peaks[k]
        if not first:
            fade = jnp.exp(state[:, channels : channels + 1] - peak)
            total = total + fade * state[:, channels + 128 : channels + 129]
            summed = summed + fade * state[:, :channels]
        out[:, :channels] = summed
        out[:, channels : channels + 128] = lanes(peak, 128)
        out[:, channels + 128 :] = lanes(total, 128)


def fold(states, own, twin, gain, blocks):
    length, channels = own.shape
    shape = ((length, channels + 256), F32)
    first = states is None
    args = (gain, own, twin, *blocks, *(() if first else states))
    kernel = functools.partial(fold_kernel, len(blocks), first)
    return call(kernel, [shape, shape], args, 24 << 20)


def spread(column, width):
    return jnp.concatenate([column] * -(-width // 128), axis=1)[:, :width]


def combine_kernel(wv_ref, wo_ref, out_ref):
    out_ref[...] = dot(wv_ref[...], wo_ref[...]).astype(BF16)


def finish_kernel(
    height, state_ref, other_ref, query_ref, last_a_ref, last_b_ref, key_gain_ref, raw_ref, partial_ref,
    wvo_ref, gain_ref, bias_ref, w_ref, hidden_ref, mixed_ref,
):
    length, channels = raw_ref.shape
    count, out = partial_ref.shape
    slots = edge_slots(count // height)
    row = lax.axis_index("rows")
    col = lax.axis_index("cols")
    has_top, has_bottom = row > 0, row < lax.axis_size("rows") - 1
    has_left, has_right = col > 0, col < lax.axis_size("cols") - 1

    keys = key_rows((last_a_ref, last_b_ref), key_gain_ref[...])
    scores = dot_t(query_ref[...], keys)
    peak_a, total_a = state_ref[:, channels : channels + 128], state_ref[:, channels + 128 :]
    peak_b, total_b = other_ref[:, channels : channels + 128], other_ref[:, channels + 128 :]
    peak = jnp.maximum(peak_a, peak_b)
    peak = jnp.maximum(peak, lanes(jnp.max(scores, axis=1, keepdims=True), 128))
    fade_a, fade_b = jnp.exp(peak_a - peak), jnp.exp(peak_b - peak)
    weights = jnp.exp(scores - spread(peak, scores.shape[1]))
    total = lanes(jnp.sum(weights, axis=1, keepdims=True), 128)
    total = total + fade_a * total_a + fade_b * total_b
    summed = dot(weights.astype(BF16), keys)
    summed = summed + spread(fade_a, channels) * state_ref[:, :channels]
    summed = summed + spread(fade_b, channels) * other_ref[:, :channels]
    pooled = (summed * spread(1.0 / total, channels)).astype(BF16)
    hidden = (raw_ref[...].astype(F32) + dot(pooled, wvo_ref[...])).astype(BF16)
    wide = hidden.astype(F32)
    value = rms_scaled(wide, gain_ref[...])
    value = value / (1.0 + jnp.exp(-value))
    slot = lax.broadcasted_iota(jnp.int32, (length, 1), 0)
    main_end = length - slots
    width = count // height
    in_top, in_bottom = slot < slots, slot >= main_end
    in_left = (slot >= slots) & (slot < slots + height)
    in_right = (slot >= main_end - height) & (slot < main_end)
    in_left = in_left | (slot == slots - 1) | (slot == length - 1)
    in_right = in_right | (slot == width) | (slot == main_end + width)
    outside = (in_top & jnp.logical_not(has_top)) | (in_bottom & jnp.logical_not(has_bottom))
    outside = outside | (in_left & jnp.logical_not(has_left)) | (in_right & jnp.logical_not(has_right))
    rows = tap_rows(jnp.where(outside, 0.0, value), height, count)

    own = hidden[slots + height : slots + height + count]
    hidden_ref[...] = own
    result = partial_ref[...] + own[:, :out].astype(F32) + bias_ref[...]
    for i in range(3):
        taps = w_ref[2, i].reshape(-1, out)
        result = result + shifted_rows(dot(rows[i], taps), i, height, count)
    mixed_ref[...] = result.astype(BF16)


def narrow(cols):
    return cols == 4


def moved(value, pairs):
    return lax.ppermute(value, AXES, pairs)


def block(
    frame_in, norm_gain, w_query, w_key, w_value, w_out, conv_gain, conv_cache, w_conv, conv_bias
):
    height, width, channels = frame_in.shape
    out_channels = w_conv.shape[4]
    count = height * width
    chips, ring, twin_pairs, down, up, cross_pairs = permutations(
        lax.axis_size("rows"), lax.axis_size("cols")
    )
    frame_far = jnp.transpose(frame_in, (1, 0, 2))
    cache_far = jnp.transpose(conv_cache, (0, 2, 1, 3))
    gain_far = norm_gain.reshape(1, channels)

    rows = edge_rows(width)
    tiles = [(frame_far.shape, BF16), (cache_far.shape, BF16), (gain_far.shape, F32)]
    far_tiles = (frame_far, cache_far, gain_far)
    edge = ((3, rows, channels), BF16)
    side = ((3, side_slots(height), channels), BF16)
    keys = ((count, channels), BF16)
    sems = [pltpu.SemaphoreType.DMA((3,))]
    hops = (chips - 1) // 2
    if narrow(lax.axis_size("cols")):
        with_row = ((count + 2 * rows, channels), BF16)
        frame, cache, gain, chain_a, to_partner = call(
            pack_chain_kernel, tiles + [with_row, with_row], (), far_args=far_tiles, scratch=sems
        )
        partner = moved(to_partner, twin_pairs)
        arrived_a = moved(chain_a, ring)
        arrived_b = moved(partner, ring)
        (chain_a,) = call(cut_kernel, [keys], (arrived_a,))
        (chain_b,) = call(cut_kernel, [keys], (arrived_b,))
        (mine,) = call(split_kernel, [((6 * rows + 2 * height, channels), BF16)], (cache, arrived_a, arrived_b))
        theirs = moved(mine, twin_pairs)
        top, bottom, twin, to_cross = call(
            sort_edges_kernel, [edge, edge, side, side], (frame, cache, partner, mine, theirs)
        )
    else:
        frame, cache, gain, first_rows, last_rows = call(
            pack_rows_kernel, tiles + [edge, edge], (), far_args=far_tiles, scratch=sems
        )
        chain_a = frame_far.reshape(count, channels)
        chain_b = moved(chain_a, twin_pairs)
        chain_a = moved(chain_a, ring)
        chain_b = moved(chain_b, ring)
        top = moved(last_rows, down)
        bottom = moved(first_rows, up)
        to_twin, to_cross = call(pack_cols_kernel, [side, side], (frame, cache, top, bottom))
        twin = moved(to_twin, twin_pairs)
    cross = moved(to_cross, cross_pairs)
    blocks = [frame, chain_a, chain_b]
    for _ in range(1, hops):
        chain_a = moved(chain_a, ring)
        chain_b = moved(chain_b, ring)
        blocks += [chain_a, chain_b]
    last_a = moved(chain_a, ring)
    last_b = moved(last_a, twin_pairs)

    far_args = (
        w_query, w_key, w_value, w_out, conv_gain.reshape(1, channels),
        conv_bias.reshape(1, out_channels), w_conv,
    )
    w_query, w_key, w_value, w_out, conv_gain, conv_bias, w_conv = far_args
    (w_both,) = call(combine_kernel, [((channels, channels), BF16)], (w_value, w_out))
    ext = ((2 * edge_slots(width) + (width + 2) * height, channels), BF16)
    raw, queries = call(query_kernel, [ext, ext], (frame, top, bottom, twin, cross, gain, w_query, w_key))
    twin_queries = moved(queries, twin_pairs)
    (partial,) = call(cache_conv_kernel, [((count, out_channels), F32)], (cache, top, bottom, twin, cross, w_conv))
    states = None
    for k in range(0, len(blocks), 7):
        states = fold(states, queries, twin_queries, gain, blocks[k : k + 7])
    other = moved(states[1], twin_pairs)
    hidden, mixed = call(
        functools.partial(finish_kernel, height),
        [((count, channels), BF16), ((count, out_channels), BF16)],
        (
            states[0], other, queries, last_a, last_b, gain, raw, partial, w_both, conv_gain, conv_bias, w_conv,
        ),
        24 << 20,
        far=True,
    )
    hidden = jnp.transpose(hidden.reshape(width, height, channels), (1, 0, 2))
    mixed = jnp.transpose(mixed.reshape(width, height, out_channels), (1, 0, 2))
    return (hidden, mixed)


def solution(mesh):
    in_specs = (
        P(("video", "rows"), "cols", None),
        P(),
        P(),
        P(),
        P(),
        P(),
        P(),
        P(None, ("video", "rows"), "cols", None),
        P(),
        P(),
    )
    out_specs = (P(("video", "rows"), "cols", None), P(("video", "rows"), "cols", None))
    return jax.shard_map(block, mesh=mesh, in_specs=in_specs, out_specs=out_specs, check_vma=False)
```

profile of v0, /device:TPU:0, one launch (start us, length us, event | category | flops | bytes accessed | tf_op | source)
XLA Modules:
  0.0 38.4 jit_solution(1830894601435516088)
XLA Ops:
  0.6 1.2 %shard_map.113 = (bf16[20,8,512]{2,1,0:T(8,128)(2,1)S(1)}, bf16[2,20,8,512]{3,2,1,0:T(8,128)(2,1)S(1)}, f32[1,512]{1,0:T(1,128)S(1)}, bf16[208,512]{1,0:T(8,128)(2,1)S(1)}, bf16[208,512]{1,0:T(8,128)(2,1)S(1)}) custom-call(bf16[20,8,512]{2,1,0:T(8,128)(2,1)} %bitcast.16, bf16[2,20,8,512]{3,2,1,0:T(8,128)(2,1)} %bitcast.15, f32[1,512]{1,0:T(1,128)} %bitcast.19), custom_call_target="tpu_custom_call" | custom-call | flops 2000000000 | bytes 4194304 | tf_op jit(solution)/shard_map/pallas_call | solution.py:25
  1.8 0.6 %collective-permute-start = (bf16[208,512]{1,0:T(8,128)(2,1)S(1)}, bf16[208,512]{1,0:T(8,128)(2,1)S(1)}, u32[]{:S(2)}, u32[]{:S(2)}) collective-permute-start(bf16[208,512]{1,0:T(8,128)(2,1)S(1)} %get-tuple-element.20), channel_id=1, source_target_pairs={{0,1},{1,0},{2,3},{3,2},{4,5},{5,4},{6,7},{7,6},{8,9},{9,8},{10,11... | collective-permute-start | bytes 638984 | tf_op jit(solution)/shard_map/ppermute | solution.py:425
  2.4 2.6 %collective-permute-start.1 = (bf16[208,512]{1,0:T(8,128)(2,1)S(1)}, bf16[208,512]{1,0:T(8,128)(2,1)S(1)}, u32[]{:S(2)}, u32[]{:S(2)}) collective-permute-start(bf16[208,512]{1,0:T(8,128)(2,1)S(1)} %get-tuple-element.21), channel_id=1, source_target_pairs={{4,8},{9,5},{8,12},{13,9},{12,14},{15,13},{14,10},{11,15},{10,6},{... | collective-permute-start | bytes 638984 | tf_op jit(solution)/shard_map/ppermute | solution.py:425
  5.0 0.0 collective-permute-done.partner_ref
  5.0 1.6 %collective-permute-start.2 = (bf16[208,512]{1,0:T(8,128)(2,1)S(1)}, bf16[208,512]{1,0:T(8,128)(2,1)S(1)}, u32[]{:S(2)}, u32[]{:S(2)}) collective-permute-start(bf16[208,512]{1,0:T(8,128)(2,1)S(1)} %collective-permute-done.partner_ref), channel_id=1, source_target_pairs={{4,8},{9,5},{8,12},{13,9},{12,14},{15,13},{14,10},{11,15},{10,6},{... | collective-permute-start | bytes 638984 | tf_op jit(solution)/shard_map/ppermute | solution.py:425
  6.6 2.2 %collective-permute-done.1.a_ref.arrived_ref = bf16[208,512]{1,0:T(8,128)(2,1)S(1)} collective-permute-done((bf16[208,512]{1,0:T(8,128)(2,1)S(1)}, bf16[208,512]{1,0:T(8,128)(2,1)S(1)}, u32[]{:S(2)}, u32[]{:S(2)}) %collective-permute-start.1) | collective-permute-done | bytes 213024 | tf_op jit(solution)/shard_map/ppermute | solution.py:425
  8.8 2.3 %collective-permute-done.2.b_ref.arrived_ref = bf16[208,512]{1,0:T(8,128)(2,1)S(1)} collective-permute-done((bf16[208,512]{1,0:T(8,128)(2,1)S(1)}, bf16[208,512]{1,0:T(8,128)(2,1)S(1)}, u32[]{:S(2)}, u32[]{:S(2)}) %collective-permute-start.2) | collective-permute-done | bytes 213024 | tf_op jit(solution)/shard_map/ppermute | solution.py:425
  11.1 0.1 shard_map.114.mine_ref
  11.2 0.1 collective-permute-start.3
  11.3 2.2 %collective-permute-start.6 = (bf16[160,512]{1,0:T(8,128)(2,1)S(1)}, bf16[160,512]{1,0:T(8,128)(2,1)S(1)}, u32[]{:S(2)}, u32[]{:S(2)}) collective-permute-start(bf16[160,512]{1,0:T(8,128)(2,1)S(1)} %shard_map.117.refs_1_), channel_id=1, source_target_pairs={{4,8},{9,5},{8,12},{13,9},{12,14},{15,13},{14,10},{11,15},{10,6},{... | collective-permute-start | bytes 491528 | tf_op jit(solution)/shard_map/ppermute | solution.py:425
  13.4 0.0 collective-permute-done.3.theirs_ref
  13.4 0.0 copy-start.2
  13.4 0.0 copy-start.3
  13.4 0.1 shard_map.115
  13.6 0.8 %collective-permute-start.4 = (bf16[3,16,512]{2,1,0:T(8,128)(2,1)S(1)}, bf16[3,16,512]{2,1,0:T(8,128)(2,1)S(1)}, u32[]{:S(2)}, u32[]{:S(2)}) collective-permute-start(bf16[3,16,512]{2,1,0:T(8,128)(2,1)S(1)} %get-tuple-element.25), channel_id=1, source_target_pairs={{1,2},{2,1},{5,6},{6,5},{9,10},{10,9},{13,14},{14,13},{17,18},{18,... | collective-permute-start | bytes 147464 | tf_op jit(solution)/shard_map/ppermute | solution.py:425
  14.4 1.6 %collective-permute-start.7 = (bf16[160,512]{1,0:T(8,128)(2,1)S(1)}, bf16[160,512]{1,0:T(8,128)(2,1)S(1)}, u32[]{:S(2)}, u32[]{:S(2)}) collective-permute-start(bf16[160,512]{1,0:T(8,128)(2,1)S(1)} %shard_map.118.refs_2_), channel_id=1, source_target_pairs={{4,8},{9,5},{8,12},{13,9},{12,14},{15,13},{14,10},{11,15},{10,6},{... | collective-permute-start | bytes 491528 | tf_op jit(solution)/shard_map/ppermute | solution.py:425
  16.0 0.0 collective-permute-done.4.cross_ref
  16.0 0.0 copy-done.2
  16.0 0.0 copy-done.3
  16.0 0.0 copy-start.4
  16.0 0.0 copy-start.5
  16.0 0.0 slice-start
  16.1 0.6 %shard_map.116 = (bf16[240,512]{1,0:T(8,128)(2,1)S(1)}, bf16[240,512]{1,0:T(8,128)(2,1)S(1)}) custom-call(bf16[20,8,512]{2,1,0:T(8,128)(2,1)S(1)} %get-tuple-element.18.frame_ref.refs_0_, bf16[3,24,512]{2,1,0:T(8,128)(2,1)S(1)} %get-tuple-element.22.top_ref, bf16[3,24,512]{2,1,0:T(8,128)(2,1)S(1)} %get-tuple-element.23.bottom_ref, ...), custom_call_target="tpu_custom_call" | custom-call | flops 2000000000 | bytes 4194304 | tf_op jit(solution)/shard_map/pallas_call | solution.py:25
  16.7 0.0 slice-start.1
  16.7 3.3 %collective-permute-start.5 = (bf16[240,512]{1,0:T(8,128)(2,1)S(1)}, bf16[240,512]{1,0:T(8,128)(2,1)S(1)}, u32[]{:S(2)}, u32[]{:S(2)}) collective-permute-start(bf16[240,512]{1,0:T(8,128)(2,1)S(1)} %get-tuple-element.26.own_ref.query_ref), channel_id=1, source_target_pairs={{0,1},{1,0},{2,3},{3,2},{4,5},{5,4},{6,7},{7,6},{8,9},{9,8},{10,11... | collective-permute-start | bytes 737288 | tf_op jit(solution)/shard_map/ppermute | solution.py:425
  19.9 0.0 collective-permute-done.6.refs_3_
  19.9 1.6 %collective-permute-start.8 = (bf16[160,512]{1,0:T(8,128)(2,1)S(1)}, bf16[160,512]{1,0:T(8,128)(2,1)S(1)}, u32[]{:S(2)}, u32[]{:S(2)}) collective-permute-start(bf16[160,512]{1,0:T(8,128)(2,1)S(1)} %collective-permute-done.6.refs_3_), channel_id=1, source_target_pairs={{4,8},{9,5},{8,12},{13,9},{12,14},{15,13},{14,10},{11,15},{10,6},{... | collective-permute-start | bytes 491528 | tf_op jit(solution)/shard_map/ppermute | solution.py:425
  21.6 0.0 collective-permute-done.7.refs_4_
  21.6 1.6 %collective-permute-start.9 = (bf16[160,512]{1,0:T(8,128)(2,1)S(1)}, bf16[160,512]{1,0:T(8,128)(2,1)S(1)}, u32[]{:S(2)}, u32[]{:S(2)}) collective-permute-start(bf16[160,512]{1,0:T(8,128)(2,1)S(1)} %collective-permute-done.7.refs_4_), channel_id=1, source_target_pairs={{4,8},{9,5},{8,12},{13,9},{12,14},{15,13},{14,10},{11,15},{10,6},{... | collective-permute-start | bytes 491528 | tf_op jit(solution)/shard_map/ppermute | solution.py:425
  23.1 2.1 %collective-permute-done.8.refs_5_ = bf16[160,512]{1,0:T(8,128)(2,1)S(1)} collective-permute-done((bf16[160,512]{1,0:T(8,128)(2,1)S(1)}, bf16[160,512]{1,0:T(8,128)(2,1)S(1)}, u32[]{:S(2)}, u32[]{:S(2)}) %collective-permute-start.8) | collective-permute-done | bytes 163872 | tf_op jit(solution)/shard_map/ppermute | solution.py:425
  25.3 1.8 %collective-permute-done.9.refs_6_ = bf16[160,512]{1,0:T(8,128)(2,1)S(1)} collective-permute-done((bf16[160,512]{1,0:T(8,128)(2,1)S(1)}, bf16[160,512]{1,0:T(8,128)(2,1)S(1)}, u32[]{:S(2)}, u32[]{:S(2)}) %collective-permute-start.9) | collective-permute-done | bytes 163872 | tf_op jit(solution)/shard_map/ppermute | solution.py:425
  27.0 0.0 collective-permute-done.5.twin_ref
  27.0 2.0 %shard_map.119 = (f32[240,768]{1,0:T(8,128)S(1)}, f32[240,768]{1,0:T(8,128)S(1)}) custom-call(f32[1,512]{1,0:T(1,128)S(1)} %get-tuple-element.17.gain_ref.key_gain_ref, bf16[240,512]{1,0:T(8,128)(2,1)S(1)} %get-tuple-element.26.own_ref.query_ref, bf16[240,512]{1,0:T(8,128)(2,1)S(1)} %collective-permute-done.5.twin_ref, ...), custom_call_target="tpu_custom_call" | custom-call | flops 2000000000 | bytes 4194304 | tf_op jit(solution)/shard_map/pallas_call | solution.py:25
  29.0 0.0 copy-start
  29.0 0.0 copy-start.1
  29.0 0.1 collective-permute-start.10
  29.1 1.7 %collective-permute-start.11 = (bf16[160,512]{1,0:T(8,128)(2,1)S(1)}, bf16[160,512]{1,0:T(8,128)(2,1)S(1)}, u32[]{:S(2)}, u32[]{:S(2)}) collective-permute-start(bf16[160,512]{1,0:T(8,128)(2,1)S(1)} %collective-permute-done.8.refs_5_), channel_id=1, source_target_pairs={{4,8},{9,5},{8,12},{13,9},{12,14},{15,13},{14,10},{11,15},{10,6},{... | collective-permute-start | bytes 491528 | tf_op jit(solution)/shard_map/ppermute | solution.py:425
  30.8 0.0 copy-done.4
  30.8 0.0 copy-done.5
  30.8 0.4 %shard_map.121.wvo_ref = bf16[512,512]{1,0:T(8,128)(2,1)S(1)} custom-call(bf16[512,512]{1,0:T(8,128)(2,1)S(1)} %copy-done.4, bf16[512,512]{1,0:T(8,128)(2,1)S(1)} %copy-done.5), custom_call_target="tpu_custom_call" | custom-call | flops 2000000000 | bytes 4194304 | tf_op jit(solution)/shard_map/pallas_call | solution.py:25
  31.2 3.3 %collective-permute-done.11.last_a_ref = bf16[160,512]{1,0:T(8,128)(2,1)S(1)} collective-permute-done((bf16[160,512]{1,0:T(8,128)(2,1)S(1)}, bf16[160,512]{1,0:T(8,128)(2,1)S(1)}, u32[]{:S(2)}, u32[]{:S(2)}) %collective-permute-start.11) | collective-permute-done | bytes 163872 | tf_op jit(solution)/shard_map/ppermute | solution.py:425
  34.5 0.0 collective-permute-start.12
  34.5 0.0 slice-done
  34.5 0.0 slice-done.1
  34.5 1.1 %shard_map.120.partial_ref = f32[160,256]{1,0:T(8,128)S(1)} custom-call(bf16[2,20,8,512]{3,2,1,0:T(8,128)(2,1)S(1)} %get-tuple-element.19.cache_ref, bf16[3,24,512]{2,1,0:T(8,128)(2,1)S(1)} %get-tuple-element.22.top_ref, bf16[3,24,512]{2,1,0:T(8,128)(2,1)S(1)} %get-tuple-element.23.bottom_ref, bf16[3,16,512]{2,1,0:T(8,128)(2,1)S(1)} %get-tuple-element.24.twin_ref, ...), custom_call_target="tpu_custom_call" | custom-call | flops 2000000000 | bytes 4194304 | tf_op jit(solution)/shard_map/pallas_call | solution.py:25
  35.6 0.3 collective-permute-done.12.last_b_ref
  35.9 0.0 collective-permute-done.10.other_ref
  35.9 0.0 copy-done
  35.9 0.0 copy-done.1
  35.9 2.6 %shard_map.122 = (bf16[160,512]{1,0:T(8,128)(2,1)}, bf16[160,256]{1,0:T(8,128)(2,1)}) custom-call(f32[240,768]{1,0:T(8,128)S(1)} %get-tuple-element.27.state_ref, f32[240,768]{1,0:T(8,128)S(1)} %collective-permute-done.10.other_ref, bf16[240,512]{1,0:T(8,128)(2,1)S(1)} %get-tuple-element.26.own_ref.query_ref, ...), custom_call_target="tpu_custom_call" | custom-call | flops 2000000000 | bytes 4194304 | tf_op jit(solution)/shard_map/pallas_call | solution.py:25
  (3 shorter events, 0.0 us)
Async XLA Ops:
  1.8 3.2 %collective-permute-start = (bf16[208,512]{1,0:T(8,128)(2,1)S(1)}, bf16[208,512]{1,0:T(8,128)(2,1)S(1)}, u32[]{:S(2)}, u32[]{:S(2)}) collective-permute-start(bf16[208,512]{1,0:T(8,128)(2,1)S(1)} %get-tuple-element.20), channel_id=1, source_target_pairs={{0,1},{1,0},{2,3},{3,2},{4,5},{5,4},{6,7},{7,6},{8,9},{9,8},{10,11... | collective-permute-start | bytes 638984 | tf_op jit(solution)/shard_map/ppermute | solution.py:425
  2.4 6.4 %collective-permute-start.1 = (bf16[208,512]{1,0:T(8,128)(2,1)S(1)}, bf16[208,512]{1,0:T(8,128)(2,1)S(1)}, u32[]{:S(2)}, u32[]{:S(2)}) collective-permute-start(bf16[208,512]{1,0:T(8,128)(2,1)S(1)} %get-tuple-element.21), channel_id=1, source_target_pairs={{4,8},{9,5},{8,12},{13,9},{12,14},{15,13},{14,10},{11,15},{10,6},{... | collective-permute-start | bytes 638984 | tf_op jit(solution)/shard_map/ppermute | solution.py:425
  5.0 6.0 %collective-permute-start.2 = (bf16[208,512]{1,0:T(8,128)(2,1)S(1)}, bf16[208,512]{1,0:T(8,128)(2,1)S(1)}, u32[]{:S(2)}, u32[]{:S(2)}) collective-permute-start(bf16[208,512]{1,0:T(8,128)(2,1)S(1)} %collective-permute-done.partner_ref), channel_id=1, source_target_pairs={{4,8},{9,5},{8,12},{13,9},{12,14},{15,13},{14,10},{11,15},{10,6},{... | collective-permute-start | bytes 638984 | tf_op jit(solution)/shard_map/ppermute | solution.py:425
  11.2 2.3 %collective-permute-start.3 = (bf16[160,512]{1,0:T(8,128)(2,1)S(1)}, bf16[160,512]{1,0:T(8,128)(2,1)S(1)}, u32[]{:S(2)}, u32[]{:S(2)}) collective-permute-start(bf16[160,512]{1,0:T(8,128)(2,1)S(1)} %shard_map.114.mine_ref), channel_id=1, source_target_pairs={{0,1},{1,0},{2,3},{3,2},{4,5},{5,4},{6,7},{7,6},{8,9},{9,8},{10,11... | collective-permute-start | bytes 491528 | tf_op jit(solution)/shard_map/ppermute | solution.py:425
  11.3 8.7 %collective-permute-start.6 = (bf16[160,512]{1,0:T(8,128)(2,1)S(1)}, bf16[160,512]{1,0:T(8,128)(2,1)S(1)}, u32[]{:S(2)}, u32[]{:S(2)}) collective-permute-start(bf16[160,512]{1,0:T(8,128)(2,1)S(1)} %shard_map.117.refs_1_), channel_id=1, source_target_pairs={{4,8},{9,5},{8,12},{13,9},{12,14},{15,13},{14,10},{11,15},{10,6},{... | collective-permute-start | bytes 491528 | tf_op jit(solution)/shard_map/ppermute | solution.py:425
  13.4 2.6 %copy-start.2 = (bf16[512,512]{1,0:T(8,128)(2,1)S(1)}, bf16[512,512]{1,0:T(8,128)(2,1)}, u32[]{:S(2)}) copy-start(bf16[512,512]{1,0:T(8,128)(2,1)} %wq_ref.1) | copy-start | bytes 1572868
  13.4 2.6 %copy-start.3 = (bf16[512,512]{1,0:T(8,128)(2,1)S(1)}, bf16[512,512]{1,0:T(8,128)(2,1)}, u32[]{:S(2)}) copy-start(bf16[512,512]{1,0:T(8,128)(2,1)} %wk_ref.1) | copy-start | bytes 1572868
  13.6 2.5 %collective-permute-start.4 = (bf16[3,16,512]{2,1,0:T(8,128)(2,1)S(1)}, bf16[3,16,512]{2,1,0:T(8,128)(2,1)S(1)}, u32[]{:S(2)}, u32[]{:S(2)}) collective-permute-start(bf16[3,16,512]{2,1,0:T(8,128)(2,1)S(1)} %get-tuple-element.25), channel_id=1, source_target_pairs={{1,2},{2,1},{5,6},{6,5},{9,10},{10,9},{13,14},{14,13},{17,18},{18,... | collective-permute-start | bytes 147464 | tf_op jit(solution)/shard_map/ppermute | solution.py:425
  14.4 7.2 %collective-permute-start.7 = (bf16[160,512]{1,0:T(8,128)(2,1)S(1)}, bf16[160,512]{1,0:T(8,128)(2,1)S(1)}, u32[]{:S(2)}, u32[]{:S(2)}) collective-permute-start(bf16[160,512]{1,0:T(8,128)(2,1)S(1)} %shard_map.118.refs_2_), channel_id=1, source_target_pairs={{4,8},{9,5},{8,12},{13,9},{12,14},{15,13},{14,10},{11,15},{10,6},{... | collective-permute-start | bytes 491528 | tf_op jit(solution)/shard_map/ppermute | solution.py:425
  16.0 14.7 %copy-start.4 = (bf16[512,512]{1,0:T(8,128)(2,1)S(1)}, bf16[512,512]{1,0:T(8,128)(2,1)}, u32[]{:S(2)}) copy-start(bf16[512,512]{1,0:T(8,128)(2,1)} %wv_ref.1) | copy-start | bytes 1572868
  16.0 14.7 %copy-start.5 = (bf16[512,512]{1,0:T(8,128)(2,1)S(1)}, bf16[512,512]{1,0:T(8,128)(2,1)}, u32[]{:S(2)}) copy-start(bf16[512,512]{1,0:T(8,128)(2,1)} %wo_ref.1) | copy-start | bytes 1572868
  16.0 18.4 %slice-start = ((s8[7077888]{0:T(1024)(128)(4,1)}), s8[4194304]{0:T(1024)(128)(4,1)S(1)}, s32[]{:S(2)}) async-start(s8[7077888]{0:T(1024)(128)(4,1)} %bitcast.11), calls=%async_computation | async-start | bytes 8388608
  16.7 17.8 %slice-start.1 = ((s8[7077888]{0:T(1024)(128)(4,1)}), s8[2883584]{0:T(1024)(128)(4,1)S(1)}, s32[]{:S(2)}) async-start(s8[7077888]{0:T(1024)(128)(4,1)} %bitcast.11), calls=%async_computation.1 | async-start | bytes 5767168
  16.7 10.3 %collective-permute-start.5 = (bf16[240,512]{1,0:T(8,128)(2,1)S(1)}, bf16[240,512]{1,0:T(8,128)(2,1)S(1)}, u32[]{:S(2)}, u32[]{:S(2)}) collective-permute-start(bf16[240,512]{1,0:T(8,128)(2,1)S(1)} %get-tuple-element.26.own_ref.query_ref), channel_id=1, source_target_pairs={{0,1},{1,0},{2,3},{3,2},{4,5},{5,4},{6,7},{7,6},{8,9},{9,8},{10,11... | collective-permute-start | bytes 737288 | tf_op jit(solution)/shard_map/ppermute | solution.py:425
  19.9 5.3 %collective-permute-start.8 = (bf16[160,512]{1,0:T(8,128)(2,1)S(1)}, bf16[160,512]{1,0:T(8,128)(2,1)S(1)}, u32[]{:S(2)}, u32[]{:S(2)}) collective-permute-start(bf16[160,512]{1,0:T(8,128)(2,1)S(1)} %collective-permute-done.6.refs_3_), channel_id=1, source_target_pairs={{4,8},{9,5},{8,12},{13,9},{12,14},{15,13},{14,10},{11,15},{10,6},{... | collective-permute-start | bytes 491528 | tf_op jit(solution)/shard_map/ppermute | solution.py:425
  21.6 5.5 %collective-permute-start.9 = (bf16[160,512]{1,0:T(8,128)(2,1)S(1)}, bf16[160,512]{1,0:T(8,128)(2,1)S(1)}, u32[]{:S(2)}, u32[]{:S(2)}) collective-permute-start(bf16[160,512]{1,0:T(8,128)(2,1)S(1)} %collective-permute-done.7.refs_4_), channel_id=1, source_target_pairs={{4,8},{9,5},{8,12},{13,9},{12,14},{15,13},{14,10},{11,15},{10,6},{... | collective-permute-start | bytes 491528 | tf_op jit(solution)/shard_map/ppermute | solution.py:425
  29.0 6.9 %copy-start = (f32[512]{0:T(512)S(1)}, f32[512]{0:T(512)}, u32[]{:S(2)}) copy-start(f32[512]{0:T(512)} %param.16) | copy-start | bytes 6148
  29.0 6.9 %copy-start.1 = (f32[256]{0:T(256)S(1)}, f32[256]{0:T(256)}, u32[]{:S(2)}) copy-start(f32[256]{0:T(256)} %param.19) | copy-start | bytes 3076
  29.0 6.8 %collective-permute-start.10 = (f32[240,768]{1,0:T(8,128)S(1)}, f32[240,768]{1,0:T(8,128)S(1)}, u32[]{:S(2)}, u32[]{:S(2)}) collective-permute-start(f32[240,768]{1,0:T(8,128)S(1)} %get-tuple-element.28), channel_id=1, source_target_pairs={{0,1},{1,0},{2,3},{3,2},{4,5},{5,4},{6,7},{7,6},{8,9},{9,8},{10,11... | collective-permute-start | bytes 2211848 | tf_op jit(solution)/shard_map/ppermute | solution.py:425
  29.1 5.4 %collective-permute-start.11 = (bf16[160,512]{1,0:T(8,128)(2,1)S(1)}, bf16[160,512]{1,0:T(8,128)(2,1)S(1)}, u32[]{:S(2)}, u32[]{:S(2)}) collective-permute-start(bf16[160,512]{1,0:T(8,128)(2,1)S(1)} %collective-permute-done.8.refs_5_), channel_id=1, source_target_pairs={{4,8},{9,5},{8,12},{13,9},{12,14},{15,13},{14,10},{11,15},{10,6},{... | collective-permute-start | bytes 491528 | tf_op jit(solution)/shard_map/ppermute | solution.py:425
  34.5 1.4 %collective-permute-start.12 = (bf16[160,512]{1,0:T(8,128)(2,1)S(1)}, bf16[160,512]{1,0:T(8,128)(2,1)S(1)}, u32[]{:S(2)}, u32[]{:S(2)}) collective-permute-start(bf16[160,512]{1,0:T(8,128)(2,1)S(1)} %collective-permute-done.11.last_a_ref), channel_id=1, source_target_pairs={{0,1},{1,0},{2,3},{3,2},{4,5},{5,4},{6,7},{7,6},{8,9},{9,8},{10,11... | collective-permute-start | bytes 491528 | tf_op jit(solution)/shard_map/ppermute | solution.py:425
where the time goes:
time: 38.6 us; the launch traced here: 38.4 us
  starting transfers between devices  17.6 us (46%)
  waiting for transfers between devices  11.9 us (31%)
  Pallas kernels  8.16 us (21%)
  between operations  0.79 us (2%)
    ppermute x13, starting transfers between devices, moved(): return lax.ppermute(value, AXES, pairs)  17.6 us
    ppermute x13, waiting for transfers between devices, moved(): return lax.ppermute(value, AXES, pairs)  11.9 us
    pallas_call x10, Pallas kernels, call(): pl.pallas_call(kernel, in_specs=[VM] * len(args) + [pl.BlockSpec(memory_s...  8.16 us
  transfers between devices with their start and end apart: 13, of which 6 were waited for; matrix products, arithmetic and copies ran while one was open for 0% of the time, Pallas kernels for 6%

commit v1 on v0

--- a/solution.py
+++ b/solution.py
@@ -67,7 +67,7 @@
 
 
 def edge_slots(width):
-    return -(-(width + 2) // 16) * 16
+    return -(-(width + 2) // 8) * 8
 
 
 def edge_rows(width):
@@ -222,10 +222,11 @@
     width = own.shape[0] // height
     slots = edge_slots(width)
     slot = lax.broadcasted_iota(jnp.int32, (slots, own.shape[1]), 0)
-    fill = jnp.zeros((slots - top.shape[0], own.shape[1]), F32)
+    spare = slots - top.shape[0]
 
     def edge(row, k):
-        row = jnp.concatenate([row, fill], axis=0)
+        if spare:
+            row = jnp.concatenate([row, jnp.zeros((spare, own.shape[1]), F32)], axis=0)
         row = jnp.where(slot == width, right[k : k + 1, :], row)
         return jnp.where(slot == slots - 1, left[k : k + 1, :], row)
 
@@ -292,7 +293,7 @@
 
 
 def query_kernel(
-    frame_ref, top_ref, bottom_ref, twin_ref, cross_ref, gain_ref, wq_ref, wk_ref, raw_ref, keys_ref
+    frame_ref, top_ref, bottom_ref, twin_ref, cross_ref, gain_ref, wqk_ref, raw_ref, keys_ref
 ):
     width, height, channels = frame_ref.shape
     odd = lax.rem(lax.axis_index("cols"), 2)
@@ -306,8 +307,7 @@
     )
     raw_ref[...] = tokens.astype(BF16)
     normed = rms_scaled(tokens, gain_ref[...]).astype(BF16)
-    rows = (dot(normed, wq_ref[...]) * (1.0 / math.sqrt(channels))).astype(BF16)
-    keys_ref[...] = dot_t(rows, wk_ref[...]).astype(BF16)
+    keys_ref[...] = (dot(normed, wqk_ref[...]) * (1.0 / math.sqrt(channels))).astype(BF16)
 
 
 def lanes(value, width):
@@ -321,9 +321,10 @@
     return parts[0] if len(parts) == 1 else jnp.concatenate(parts, axis=0)
 
 
-def fold_kernel(blocks, first, gain_ref, own_ref, twin_ref, *refs):
+def fold_kernel(blocks, first, last, gain_ref, own_ref, twin_ref, *refs):
     keys = key_rows(refs[:blocks], gain_ref[...])
-    states, outs = ((None, None), refs[blocks:]) if first else (refs[blocks:-2], refs[-2:])
+    refs = refs[blocks:]
+    states, outs = ((None, None), refs) if first else (refs[:2], refs[2:])
     channels = keys.shape[1]
     length = own_ref.shape[0]
     all_scores = dot_t(jnp.concatenate([own_ref[...], twin_ref[...]], axis=0), keys)
@@ -344,30 +345,52 @@
             fade = jnp.exp(state[:, channels : channels + 1] - peak)
             total = total + fade * state[:, channels + 128 : channels + 129]
             summed = summed + fade * state[:, :channels]
-        out[:, :channels] = summed
-        out[:, channels : channels + 128] = lanes(peak, 128)
-        out[:, channels + 128 :] = lanes(total, 128)
-
-
-def fold(states, own, twin, gain, blocks):
+        if last and k == 1:
+            out[...] = summed.astype(BF16)
+            outs[2][:, :128] = lanes(peak, 128)
+            outs[2][:, 128:] = lanes(total, 128)
+        else:
+            out[:, :channels] = summed
+            out[:, channels : channels + 128] = lanes(peak, 128)
+            out[:, channels + 128 :] = lanes(total, 128)
+
+
+def fold(states, own, twin, gain, blocks, last):
     length, channels = own.shape
     shape = ((length, channels + 256), F32)
     first = states is None
     args = (gain, own, twin, *blocks, *(() if first else states))
-    kernel = functools.partial(fold_kernel, len(blocks), first)
-    return call(kernel, [shape, shape], args, 24 << 20)
+    kernel = functools.partial(fold_kernel, len(blocks), first, last)
+    others = [((length, channels), BF16), ((length, 256), F32)] if last else [shape]
+    return call(kernel, [shape, *others], args, 24 << 20)
 
 
 def spread(column, width):
     return jnp.concatenate([column] * -(-width // 128), axis=1)[:, :width]
 
 
-def combine_kernel(wv_ref, wo_ref, out_ref):
-    out_ref[...] = dot(wv_ref[...], wo_ref[...]).astype(BF16)
+def fold_own_kernel(gain_ref, query_ref, block_ref, state_ref, out_ref):
+    keys = key_rows((block_ref,), gain_ref[...])
+    channels = keys.shape[1]
+    scores = dot_t(query_ref[...], keys)
+    before = state_ref[:, channels : channels + 128]
+    peak = jnp.maximum(before, lanes(jnp.max(scores, axis=1, keepdims=True), 128))
+    fade = jnp.exp(before - peak)
+    weights = jnp.exp(scores - spread(peak, scores.shape[1]))
+    total = lanes(jnp.sum(weights, axis=1, keepdims=True), 128)
+    summed = dot(weights.astype(BF16), keys)
+    out_ref[:, :channels] = summed + spread(fade, channels) * state_ref[:, :channels]
+    out_ref[:, channels : channels + 128] = peak
+    out_ref[:, channels + 128 :] = total + fade * state_ref[:, channels + 128 :]
+
+
+def combine_kernel(wq_ref, wk_ref, wv_ref, wo_ref, query_key_ref, value_out_ref):
+    query_key_ref[...] = dot_t(wq_ref[...], wk_ref[...]).astype(BF16)
+    value_out_ref[...] = dot(wv_ref[...], wo_ref[...]).astype(BF16)
 
 
 def finish_kernel(
-    height, state_ref, other_ref, query_ref, last_a_ref, last_b_ref, key_gain_ref, raw_ref, partial_ref,
+    height, state_ref, other_ref, scale_ref, query_ref, last_ref, key_gain_ref, raw_ref, partial_ref,
     wvo_ref, gain_ref, bias_ref, w_ref, hidden_ref, mixed_ref,
 ):
     length, channels = raw_ref.shape
@@ -378,10 +401,10 @@
     has_top, has_bottom = row > 0, row < lax.axis_size("rows") - 1
     has_left, has_right = col > 0, col < lax.axis_size("cols") - 1
 
-    keys = key_rows((last_a_ref, last_b_ref), key_gain_ref[...])
+    keys = key_rows((last_ref,), key_gain_ref[...])
     scores = dot_t(query_ref[...], keys)
     peak_a, total_a = state_ref[:, channels : channels + 128], state_ref[:, channels + 128 :]
-    peak_b, total_b = other_ref[:, channels : channels + 128], other_ref[:, channels + 128 :]
+    peak_b, total_b = scale_ref[:, :128], scale_ref[:, 128:]
     peak = jnp.maximum(peak_a, peak_b)
     peak = jnp.maximum(peak, lanes(jnp.max(scores, axis=1, keepdims=True), 128))
     fade_a, fade_b = jnp.exp(peak_a - peak), jnp.exp(peak_b - peak)
@@ -390,7 +413,7 @@
     total = total + fade_a * total_a + fade_b * total_b
     summed = dot(weights.astype(BF16), keys)
     summed = summed + spread(fade_a, channels) * state_ref[:, :channels]
-    summed = summed + spread(fade_b, channels) * other_ref[:, :channels]
+    summed = summed + spread(fade_b, channels) * other_ref[...].astype(F32)
     pooled = (summed * spread(1.0 / total, channels)).astype(BF16)
     hidden = (raw_ref[...].astype(F32) + dot(pooled, wvo_ref[...])).astype(BF16)
     wide = hidden.astype(F32)
@@ -487,20 +510,23 @@
         conv_bias.reshape(1, out_channels), w_conv,
     )
     w_query, w_key, w_value, w_out, conv_gain, conv_bias, w_conv = far_args
-    (w_both,) = call(combine_kernel, [((channels, channels), BF16)], (w_value, w_out))
+    square = ((channels, channels), BF16)
+    w_query_key, w_value_out = call(combine_kernel, [square, square], (w_query, w_key, w_value, w_out))
     ext = ((2 * edge_slots(width) + (width + 2) * height, channels), BF16)
-    raw, queries = call(query_kernel, [ext, ext], (frame, top, bottom, twin, cross, gain, w_query, w_key))
+    raw, queries = call(query_kernel, [ext, ext], (frame, top, bottom, twin, cross, gain, w_query_key))
     twin_queries = moved(queries, twin_pairs)
     (partial,) = call(cache_conv_kernel, [((count, out_channels), F32)], (cache, top, bottom, twin, cross, w_conv))
     states = None
     for k in range(0, len(blocks), 7):
-        states = fold(states, queries, twin_queries, gain, blocks[k : k + 7])
+        states = fold(states, queries, twin_queries, gain, blocks[k : k + 7], k + 7 >= len(blocks))
     other = moved(states[1], twin_pairs)
+    other_scale = moved(states[2], twin_pairs)
+    (state,) = call(fold_own_kernel, [(states[0].shape, F32)], (gain, queries, last_a, states[0]))
     hidden, mixed = call(
         functools.partial(finish_kernel, height),
         [((count, channels), BF16), ((count, out_channels), BF16)],
         (
-            states[0], other, queries, last_a, last_b, gain, raw, partial, w_both, conv_gain, conv_bias, w_conv,
+            state, other, other_scale, queries, last_b, gain, raw, partial, w_value_out, conv_gain, conv_bias, w_conv,
         ),
         24 << 20,
         far=True,

time: 38.6 us -> 34.3 us (0.89)
  waiting for transfers between devices: 11.9 us -> 6.62 us
  starting transfers between devices: 17.6 us -> 18.1 us
  Pallas kernels: 8.16 us -> 8.62 us
    ppermute x13 -> x14, waiting for transfers between devices: 11.9 us -> 6.62 us  [moved(): return lax.ppermute(value, AXES, pairs)]
    ppermute x13 -> x14, starting transfers between devices: 17.6 us -> 18.1 us  [moved(): return lax.ppermute(value, AXES, pairs)]
    pallas_call x10 -> x11, Pallas kernels: 8.16 us -> 8.62 us  [call(): pl.pallas_call(kernel, in_specs=[VM] * len(args) + [pl.BlockSpec(memory_s...]
  transfers between devices with their start and end apart: 13 -> 14, of which waited for: 6 -> 5; matrix products, arithmetic and copies ran while one was open for 0% -> 0% of each run, Pallas kernels for 6% -> 14%
where the time goes in v1:
time: 34.3 us; the launch traced here: 34.2 us
  starting transfers between devices  18.1 us (53%)
  Pallas kernels  8.62 us (25%)
  waiting for transfers between devices  6.62 us (19%)
  between operations  0.8 us (2%)
    ppermute x14, starting transfers between devices, moved(): return lax.ppermute(value, AXES, pairs)  18.1 us
    pallas_call x11, Pallas kernels, call(): pl.pallas_call(kernel, in_specs=[VM] * len(args) + [pl.BlockSpec(memory_s...  8.62 us
    ppermute x14, waiting for transfers between devices, moved(): return lax.ppermute(value, AXES, pairs)  6.62 us
  transfers between devices with their start and end apart: 14, of which 5 were waited for; matrix products, arithmetic and copies ran while one was open for 0% of the time, Pallas kernels for 14%

profile of v1, /device:TPU:0, one launch (start us, length us, event | category | flops | bytes accessed | tf_op | source)
XLA Modules:
  0.0 34.2 jit_solution(10550023747892775703)
XLA Ops:
  0.6 0.0 copy-start.2
  0.6 0.0 copy-start.3
  0.7 0.0 copy-start.4
  0.7 0.0 copy-start.5
  0.7 1.3 %shard_map.113 = (bf16[20,8,512]{2,1,0:T(8,128)(2,1)S(1)}, bf16[2,20,8,512]{3,2,1,0:T(8,128)(2,1)S(1)}, f32[1,512]{1,0:T(1,128)S(1)}, bf16[208,512]{1,0:T(8,128)(2,1)S(1)}, bf16[208,512]{1,0:T(8,128)(2,1)S(1)}) custom-call(bf16[20,8,512]{2,1,0:T(8,128)(2,1)} %bitcast.16, bf16[2,20,8,512]{3,2,1,0:T(8,128)(2,1)} %bitcast.15, f32[1,512]{1,0:T(1,128)} %bitcast.19), custom_call_target="tpu_custom_call" | custom-call | flops 2000000000 | bytes 4194304 | tf_op jit(solution)/shard_map/pallas_call | solution.py:25
  2.0 0.6 %collective-permute-start = (bf16[208,512]{1,0:T(8,128)(2,1)S(1)}, bf16[208,512]{1,0:T(8,128)(2,1)S(1)}, u32[]{:S(2)}, u32[]{:S(2)}) collective-permute-start(bf16[208,512]{1,0:T(8,128)(2,1)S(1)} %get-tuple-element.23), channel_id=1, source_target_pairs={{0,1},{1,0},{2,3},{3,2},{4,5},{5,4},{6,7},{7,6},{8,9},{9,8},{10,11... | collective-permute-start | bytes 638984 | tf_op jit(solution)/shard_map/ppermute | solution.py:448
  2.6 2.6 %collective-permute-start.1 = (bf16[208,512]{1,0:T(8,128)(2,1)S(1)}, bf16[208,512]{1,0:T(8,128)(2,1)S(1)}, u32[]{:S(2)}, u32[]{:S(2)}) collective-permute-start(bf16[208,512]{1,0:T(8,128)(2,1)S(1)} %get-tuple-element.24), channel_id=1, source_target_pairs={{4,8},{9,5},{8,12},{13,9},{12,14},{15,13},{14,10},{11,15},{10,6},{... | collective-permute-start | bytes 638984 | tf_op jit(solution)/shard_map/ppermute | solution.py:448
  5.2 0.0 collective-permute-done.partner_ref
  5.2 1.6 %collective-permute-start.2 = (bf16[208,512]{1,0:T(8,128)(2,1)S(1)}, bf16[208,512]{1,0:T(8,128)(2,1)S(1)}, u32[]{:S(2)}, u32[]{:S(2)}) collective-permute-start(bf16[208,512]{1,0:T(8,128)(2,1)S(1)} %collective-permute-done.partner_ref), channel_id=1, source_target_pairs={{4,8},{9,5},{8,12},{13,9},{12,14},{15,13},{14,10},{11,15},{10,6},{... | collective-permute-start | bytes 638984 | tf_op jit(solution)/shard_map/ppermute | solution.py:448
  6.8 0.0 copy-done.2
  6.8 0.0 copy-done.3
  6.8 0.0 copy-done.4
  6.8 0.0 copy-done.5
  6.8 0.7 %shard_map.116 = (bf16[512,512]{1,0:T(8,128)(2,1)S(1)}, bf16[512,512]{1,0:T(8,128)(2,1)S(1)}) custom-call(bf16[512,512]{1,0:T(8,128)(2,1)S(1)} %copy-done.2, bf16[512,512]{1,0:T(8,128)(2,1)S(1)} %copy-done.3, bf16[512,512]{1,0:T(8,128)(2,1)S(1)} %copy-done.4, bf16[512,512]{1,0:T(8,128)(2,1)S(1)} %copy-done.5), custom_call_target="tpu_custom_call" | custom-call | flops 2000000000 | bytes 4194304 | tf_op jit(solution)/shard_map/pallas_call | solution.py:25
  7.5 1.4 %collective-permute-done.1.a_ref.arrived_ref = bf16[208,512]{1,0:T(8,128)(2,1)S(1)} collective-permute-done((bf16[208,512]{1,0:T(8,128)(2,1)S(1)}, bf16[208,512]{1,0:T(8,128)(2,1)S(1)}, u32[]{:S(2)}, u32[]{:S(2)}) %collective-permute-start.1) | collective-permute-done | bytes 213024 | tf_op jit(solution)/shard_map/ppermute | solution.py:448
  8.9 2.3 %collective-permute-done.2.b_ref.arrived_ref = bf16[208,512]{1,0:T(8,128)(2,1)S(1)} collective-permute-done((bf16[208,512]{1,0:T(8,128)(2,1)S(1)}, bf16[208,512]{1,0:T(8,128)(2,1)S(1)}, u32[]{:S(2)}, u32[]{:S(2)}) %collective-permute-start.2) | collective-permute-done | bytes 213024 | tf_op jit(solution)/shard_map/ppermute | solution.py:448
  11.2 0.1 shard_map.114.mine_ref
  11.3 0.1 collective-permute-start.3
  11.4 2.2 %collective-permute-start.5 = (bf16[160,512]{1,0:T(8,128)(2,1)S(1)}, bf16[160,512]{1,0:T(8,128)(2,1)S(1)}, u32[]{:S(2)}, u32[]{:S(2)}) collective-permute-start(bf16[160,512]{1,0:T(8,128)(2,1)S(1)} %shard_map.118.refs_1_), channel_id=1, source_target_pairs={{4,8},{9,5},{8,12},{13,9},{12,14},{15,13},{14,10},{11,15},{10,6},{... | collective-permute-start | bytes 491528 | tf_op jit(solution)/shard_map/ppermute | solution.py:448
  13.6 0.0 collective-permute-done.3.theirs_ref
  13.6 0.1 shard_map.115
  13.7 0.7 %collective-permute-start.4 = (bf16[3,16,512]{2,1,0:T(8,128)(2,1)S(1)}, bf16[3,16,512]{2,1,0:T(8,128)(2,1)S(1)}, u32[]{:S(2)}, u32[]{:S(2)}) collective-permute-start(bf16[3,16,512]{2,1,0:T(8,128)(2,1)S(1)} %get-tuple-element.28), channel_id=1, source_target_pairs={{1,2},{2,1},{5,6},{6,5},{9,10},{10,9},{13,14},{14,13},{17,18},{18,... | collective-permute-start | bytes 147464 | tf_op jit(solution)/shard_map/ppermute | solution.py:448
  14.4 1.6 %collective-permute-start.9 = (bf16[160,512]{1,0:T(8,128)(2,1)S(1)}, bf16[160,512]{1,0:T(8,128)(2,1)S(1)}, u32[]{:S(2)}, u32[]{:S(2)}) collective-permute-start(bf16[160,512]{1,0:T(8,128)(2,1)S(1)} %shard_map.119.refs_2_), channel_id=1, source_target_pairs={{4,8},{9,5},{8,12},{13,9},{12,14},{15,13},{14,10},{11,15},{10,6},{... | collective-permute-start | bytes 491528 | tf_op jit(solution)/shard_map/ppermute | solution.py:448
  16.1 0.0 collective-permute-done.4.cross_ref
  16.1 0.0 slice-start
  16.1 0.0 slice-start.1
  16.1 0.4 %shard_map.117 = (bf16[224,512]{1,0:T(8,128)(2,1)S(1)}, bf16[224,512]{1,0:T(8,128)(2,1)S(1)}) custom-call(bf16[20,8,512]{2,1,0:T(8,128)(2,1)S(1)} %get-tuple-element.21.frame_ref.refs_0_, bf16[3,24,512]{2,1,0:T(8,128)(2,1)S(1)} %get-tuple-element.25.top_ref, bf16[3,24,512]{2,1,0:T(8,128)(2,1)S(1)} %get-tuple-element.26.bottom_ref, ...), custom_call_target="tpu_custom_call" | custom-call | flops 2000000000 | bytes 4194304 | tf_op jit(solution)/shard_map/pallas_call | solution.py:25
  16.4 3.3 %collective-permute-start.8 = (bf16[224,512]{1,0:T(8,128)(2,1)S(1)}, bf16[224,512]{1,0:T(8,128)(2,1)S(1)}, u32[]{:S(2)}, u32[]{:S(2)}) collective-permute-start(bf16[224,512]{1,0:T(8,128)(2,1)S(1)} %get-tuple-element.30.own_ref.query_ref), channel_id=1, source_target_pairs={{0,1},{1,0},{2,3},{3,2},{4,5},{5,4},{6,7},{7,6},{8,9},{9,8},{10,11... | collective-permute-start | bytes 688136 | tf_op jit(solution)/shard_map/ppermute | solution.py:448
  19.7 0.0 collective-permute-done.5.refs_3_
  19.7 1.6 %collective-permute-start.6 = (bf16[160,512]{1,0:T(8,128)(2,1)S(1)}, bf16[160,512]{1,0:T(8,128)(2,1)S(1)}, u32[]{:S(2)}, u32[]{:S(2)}) collective-permute-start(bf16[160,512]{1,0:T(8,128)(2,1)S(1)} %collective-permute-done.5.refs_3_), channel_id=1, source_target_pairs={{4,8},{9,5},{8,12},{13,9},{12,14},{15,13},{14,10},{11,15},{10,6},{... | collective-permute-start | bytes 491528 | tf_op jit(solution)/shard_map/ppermute | solution.py:448
  21.3 0.0 collective-permute-done.9.refs_4_
  21.3 1.6 %collective-permute-start.10 = (bf16[160,512]{1,0:T(8,128)(2,1)S(1)}, bf16[160,512]{1,0:T(8,128)(2,1)S(1)}, u32[]{:S(2)}, u32[]{:S(2)}) collective-permute-start(bf16[160,512]{1,0:T(8,128)(2,1)S(1)} %collective-permute-done.9.refs_4_), channel_id=1, source_target_pairs={{4,8},{9,5},{8,12},{13,9},{12,14},{15,13},{14,10},{11,15},{10,6},{... | collective-permute-start | bytes 491528 | tf_op jit(solution)/shard_map/ppermute | solution.py:448
  22.9 2.1 %collective-permute-done.6.refs_5_ = bf16[160,512]{1,0:T(8,128)(2,1)S(1)} collective-permute-done((bf16[160,512]{1,0:T(8,128)(2,1)S(1)}, bf16[160,512]{1,0:T(8,128)(2,1)S(1)}, u32[]{:S(2)}, u32[]{:S(2)}) %collective-permute-start.6) | collective-permute-done | bytes 163872 | tf_op jit(solution)/shard_map/ppermute | solution.py:448
  25.0 1.6 %collective-permute-start.7 = (bf16[160,512]{1,0:T(8,128)(2,1)S(1)}, bf16[160,512]{1,0:T(8,128)(2,1)S(1)}, u32[]{:S(2)}, u32[]{:S(2)}) collective-permute-start(bf16[160,512]{1,0:T(8,128)(2,1)S(1)} %collective-permute-done.6.refs_5_), channel_id=1, source_target_pairs={{4,8},{9,5},{8,12},{13,9},{12,14},{15,13},{14,10},{11,15},{10,6},{... | collective-permute-start | bytes 491528 | tf_op jit(solution)/shard_map/ppermute | solution.py:448
  26.6 0.1 collective-permute-done.10.refs_6_
  26.8 0.0 collective-permute-done.8.twin_ref
  26.8 1.9 %shard_map.120 = (f32[224,768]{1,0:T(8,128)S(1)}, bf16[224,512]{1,0:T(8,128)(2,1)S(1)}, f32[224,256]{1,0:T(8,128)S(1)}) custom-call(f32[1,512]{1,0:T(1,128)S(1)} %get-tuple-element.20.gain_ref.key_gain_ref, bf16[224,512]{1,0:T(8,128)(2,1)S(1)} %get-tuple-element.30.own_ref.query_ref, bf16[224,512]{1,0:T(8,128)(2,1)S(1)} %collective-permute-done.8.twin_ref, ...), custom_call_target="tpu_custom_call" | custom-call | flops 2000000000 | bytes 4194304 | tf_op jit(solution)/shard_map/pallas_call | solution.py:25
  28.7 0.1 collective-permute-start.11
  28.7 0.0 copy-start
  28.7 0.0 copy-start.1
  28.8 0.5 %collective-permute-start.12 = (f32[224,256]{1,0:T(8,128)S(1)}, f32[224,256]{1,0:T(8,128)S(1)}, u32[]{:S(2)}, u32[]{:S(2)}) collective-permute-start(f32[224,256]{1,0:T(8,128)S(1)} %get-tuple-element.33), channel_id=1, source_target_pairs={{0,1},{1,0},{2,3},{3,2},{4,5},{5,4},{6,7},{7,6},{8,9},{9,8},{10,11... | collective-permute-start | bytes 688136 | tf_op jit(solution)/shard_map/ppermute | solution.py:448
  29.2 0.0 slice-done
  29.2 0.0 slice-done.1
  29.2 1.1 %shard_map.122.partial_ref = f32[160,256]{1,0:T(8,128)S(1)} custom-call(bf16[2,20,8,512]{3,2,1,0:T(8,128)(2,1)S(1)} %get-tuple-element.22.cache_ref, bf16[3,24,512]{2,1,0:T(8,128)(2,1)S(1)} %get-tuple-element.25.top_ref, bf16[3,24,512]{2,1,0:T(8,128)(2,1)S(1)} %get-tuple-element.26.bottom_ref, bf16[3,16,512]{2,1,0:T(8,128)(2,1)S(1)} %get-tuple-element.27.twin_ref, ...), custom_call_target="tpu_custom_call" | custom-call | flops 2000000000 | bytes 4194304 | tf_op jit(solution)/shard_map/pallas_call | solution.py:25
  30.3 0.0 collective-permute-done.7.block_ref
  30.4 0.2 collective-permute-start.13
  30.5 0.6 %shard_map.121.state_ref = f32[224,768]{1,0:T(8,128)S(1)} custom-call(f32[1,512]{1,0:T(1,128)S(1)} %get-tuple-element.20.gain_ref.key_gain_ref, bf16[224,512]{1,0:T(8,128)(2,1)S(1)} %get-tuple-element.30.own_ref.query_ref, bf16[160,512]{1,0:T(8,128)(2,1)S(1)} %collective-permute-done.7.block_ref, f32[224,768]{1,0:T(8,128)S(1)} %get-tuple-element.31.state_ref), custom_call_target="tpu_custom_call" | custom-call | flops 2000000000 | bytes 4194304 | tf_op jit(solution)/shard_map/pallas_call | solution.py:25
  31.2 0.7 %collective-permute-done.13.last_ref = bf16[160,512]{1,0:T(8,128)(2,1)S(1)} collective-permute-done((bf16[160,512]{1,0:T(8,128)(2,1)S(1)}, bf16[160,512]{1,0:T(8,128)(2,1)S(1)}, u32[]{:S(2)}, u32[]{:S(2)}) %collective-permute-start.13) | collective-permute-done | bytes 163872 | tf_op jit(solution)/shard_map/ppermute | solution.py:448
  31.8 0.0 collective-permute-done.11.other_ref
  31.8 0.0 collective-permute-done.12.scale_ref
  31.8 0.0 copy-done
  31.8 0.0 copy-done.1
  31.8 2.3 %shard_map.123 = (bf16[160,512]{1,0:T(8,128)(2,1)}, bf16[160,256]{1,0:T(8,128)(2,1)}) custom-call(f32[224,768]{1,0:T(8,128)S(1)} %shard_map.121.state_ref, bf16[224,512]{1,0:T(8,128)(2,1)S(1)} %collective-permute-done.11.other_ref, f32[224,256]{1,0:T(8,128)S(1)} %collective-permute-done.12.scale_ref, ...), custom_call_target="tpu_custom_call" | custom-call | flops 2000000000 | bytes 4194304 | tf_op jit(solution)/shard_map/pallas_call | solution.py:25
  (3 shorter events, 0.0 us)
Async XLA Ops:
  0.6 6.2 %copy-start.2 = (bf16[512,512]{1,0:T(8,128)(2,1)S(1)}, bf16[512,512]{1,0:T(8,128)(2,1)}, u32[]{:S(2)}) copy-start(bf16[512,512]{1,0:T(8,128)(2,1)} %wq_ref.1) | copy-start | bytes 1572868
  0.6 6.1 %copy-start.3 = (bf16[512,512]{1,0:T(8,128)(2,1)S(1)}, bf16[512,512]{1,0:T(8,128)(2,1)}, u32[]{:S(2)}) copy-start(bf16[512,512]{1,0:T(8,128)(2,1)} %wk_ref.1) | copy-start | bytes 1572868
  0.7 6.1 %copy-start.4 = (bf16[512,512]{1,0:T(8,128)(2,1)S(1)}, bf16[512,512]{1,0:T(8,128)(2,1)}, u32[]{:S(2)}) copy-start(bf16[512,512]{1,0:T(8,128)(2,1)} %wv_ref.1) | copy-start | bytes 1572868
  0.7 6.1 %copy-start.5 = (bf16[512,512]{1,0:T(8,128)(2,1)S(1)}, bf16[512,512]{1,0:T(8,128)(2,1)}, u32[]{:S(2)}) copy-start(bf16[512,512]{1,0:T(8,128)(2,1)} %wo_ref.1) | copy-start | bytes 1572868
  2.0 3.2 %collective-permute-start = (bf16[208,512]{1,0:T(8,128)(2,1)S(1)}, bf16[208,512]{1,0:T(8,128)(2,1)S(1)}, u32[]{:S(2)}, u32[]{:S(2)}) collective-permute-start(bf16[208,512]{1,0:T(8,128)(2,1)S(1)} %get-tuple-element.23), channel_id=1, source_target_pairs={{0,1},{1,0},{2,3},{3,2},{4,5},{5,4},{6,7},{7,6},{8,9},{9,8},{10,11... | collective-permute-start | bytes 638984 | tf_op jit(solution)/shard_map/ppermute | solution.py:448
  2.6 6.4 %collective-permute-start.1 = (bf16[208,512]{1,0:T(8,128)(2,1)S(1)}, bf16[208,512]{1,0:T(8,128)(2,1)S(1)}, u32[]{:S(2)}, u32[]{:S(2)}) collective-permute-start(bf16[208,512]{1,0:T(8,128)(2,1)S(1)} %get-tuple-element.24), channel_id=1, source_target_pairs={{4,8},{9,5},{8,12},{13,9},{12,14},{15,13},{14,10},{11,15},{10,6},{... | collective-permute-start | bytes 638984 | tf_op jit(solution)/shard_map/ppermute | solution.py:448
  5.2 6.0 %collective-permute-start.2 = (bf16[208,512]{1,0:T(8,128)(2,1)S(1)}, bf16[208,512]{1,0:T(8,128)(2,1)S(1)}, u32[]{:S(2)}, u32[]{:S(2)}) collective-permute-start(bf16[208,512]{1,0:T(8,128)(2,1)S(1)} %collective-permute-done.partner_ref), channel_id=1, source_target_pairs={{4,8},{9,5},{8,12},{13,9},{12,14},{15,13},{14,10},{11,15},{10,6},{... | collective-permute-start | bytes 638984 | tf_op jit(solution)/shard_map/ppermute | solution.py:448
  11.3 2.3 %collective-permute-start.3 = (bf16[160,512]{1,0:T(8,128)(2,1)S(1)}, bf16[160,512]{1,0:T(8,128)(2,1)S(1)}, u32[]{:S(2)}, u32[]{:S(2)}) collective-permute-start(bf16[160,512]{1,0:T(8,128)(2,1)S(1)} %shard_map.114.mine_ref), channel_id=1, source_target_pairs={{0,1},{1,0},{2,3},{3,2},{4,5},{5,4},{6,7},{7,6},{8,9},{9,8},{10,11... | collective-permute-start | bytes 491528 | tf_op jit(solution)/shard_map/ppermute | solution.py:448
  11.4 8.3 %collective-permute-start.5 = (bf16[160,512]{1,0:T(8,128)(2,1)S(1)}, bf16[160,512]{1,0:T(8,128)(2,1)S(1)}, u32[]{:S(2)}, u32[]{:S(2)}) collective-permute-start(bf16[160,512]{1,0:T(8,128)(2,1)S(1)} %shard_map.118.refs_1_), channel_id=1, source_target_pairs={{4,8},{9,5},{8,12},{13,9},{12,14},{15,13},{14,10},{11,15},{10,6},{... | collective-permute-start | bytes 491528 | tf_op jit(solution)/shard_map/ppermute | solution.py:448
  13.7 2.3 %collective-permute-start.4 = (bf16[3,16,512]{2,1,0:T(8,128)(2,1)S(1)}, bf16[3,16,512]{2,1,0:T(8,128)(2,1)S(1)}, u32[]{:S(2)}, u32[]{:S(2)}) collective-permute-start(bf16[3,16,512]{2,1,0:T(8,128)(2,1)S(1)} %get-tuple-element.28), channel_id=1, source_target_pairs={{1,2},{2,1},{5,6},{6,5},{9,10},{10,9},{13,14},{14,13},{17,18},{18,... | collective-permute-start | bytes 147464 | tf_op jit(solution)/shard_map/ppermute | solution.py:448
  14.4 6.9 %collective-permute-start.9 = (bf16[160,512]{1,0:T(8,128)(2,1)S(1)}, bf16[160,512]{1,0:T(8,128)(2,1)S(1)}, u32[]{:S(2)}, u32[]{:S(2)}) collective-permute-start(bf16[160,512]{1,0:T(8,128)(2,1)S(1)} %shard_map.119.refs_2_), channel_id=1, source_target_pairs={{4,8},{9,5},{8,12},{13,9},{12,14},{15,13},{14,10},{11,15},{10,6},{... | collective-permute-start | bytes 491528 | tf_op jit(solution)/shard_map/ppermute | solution.py:448
  16.1 13.2 %slice-start = ((s8[7077888]{0:T(1024)(128)(4,1)}), s8[4194304]{0:T(1024)(128)(4,1)S(1)}, s32[]{:S(2)}) async-start(s8[7077888]{0:T(1024)(128)(4,1)} %bitcast.11), calls=%async_computation | async-start | bytes 8388608
  16.1 13.2 %slice-start.1 = ((s8[7077888]{0:T(1024)(128)(4,1)}), s8[2883584]{0:T(1024)(128)(4,1)S(1)}, s32[]{:S(2)}) async-start(s8[7077888]{0:T(1024)(128)(4,1)} %bitcast.11), calls=%async_computation.1 | async-start | bytes 5767168
  16.4 10.4 %collective-permute-start.8 = (bf16[224,512]{1,0:T(8,128)(2,1)S(1)}, bf16[224,512]{1,0:T(8,128)(2,1)S(1)}, u32[]{:S(2)}, u32[]{:S(2)}) collective-permute-start(bf16[224,512]{1,0:T(8,128)(2,1)S(1)} %get-tuple-element.30.own_ref.query_ref), channel_id=1, source_target_pairs={{0,1},{1,0},{2,3},{3,2},{4,5},{5,4},{6,7},{7,6},{8,9},{9,8},{10,11... | collective-permute-start | bytes 688136 | tf_op jit(solution)/shard_map/ppermute | solution.py:448
  19.7 5.3 %collective-permute-start.6 = (bf16[160,512]{1,0:T(8,128)(2,1)S(1)}, bf16[160,512]{1,0:T(8,128)(2,1)S(1)}, u32[]{:S(2)}, u32[]{:S(2)}) collective-permute-start(bf16[160,512]{1,0:T(8,128)(2,1)S(1)} %collective-permute-done.5.refs_3_), channel_id=1, source_target_pairs={{4,8},{9,5},{8,12},{13,9},{12,14},{15,13},{14,10},{11,15},{10,6},{... | collective-permute-start | bytes 491528 | tf_op jit(solution)/shard_map/ppermute | solution.py:448
  21.3 5.5 %collective-permute-start.10 = (bf16[160,512]{1,0:T(8,128)(2,1)S(1)}, bf16[160,512]{1,0:T(8,128)(2,1)S(1)}, u32[]{:S(2)}, u32[]{:S(2)}) collective-permute-start(bf16[160,512]{1,0:T(8,128)(2,1)S(1)} %collective-permute-done.9.refs_4_), channel_id=1, source_target_pairs={{4,8},{9,5},{8,12},{13,9},{12,14},{15,13},{14,10},{11,15},{10,6},{... | collective-permute-start | bytes 491528 | tf_op jit(solution)/shard_map/ppermute | solution.py:448
  25.0 5.3 %collective-permute-start.7 = (bf16[160,512]{1,0:T(8,128)(2,1)S(1)}, bf16[160,512]{1,0:T(8,128)(2,1)S(1)}, u32[]{:S(2)}, u32[]{:S(2)}) collective-permute-start(bf16[160,512]{1,0:T(8,128)(2,1)S(1)} %collective-permute-done.6.refs_5_), channel_id=1, source_target_pairs={{4,8},{9,5},{8,12},{13,9},{12,14},{15,13},{14,10},{11,15},{10,6},{... | collective-permute-start | bytes 491528 | tf_op jit(solution)/shard_map/ppermute | solution.py:448
  28.7 3.2 %collective-permute-start.11 = (bf16[224,512]{1,0:T(8,128)(2,1)S(1)}, bf16[224,512]{1,0:T(8,128)(2,1)S(1)}, u32[]{:S(2)}, u32[]{:S(2)}) collective-permute-start(bf16[224,512]{1,0:T(8,128)(2,1)S(1)} %get-tuple-element.32), channel_id=1, source_target_pairs={{0,1},{1,0},{2,3},{3,2},{4,5},{5,4},{6,7},{7,6},{8,9},{9,8},{10,11... | collective-permute-start | bytes 688136 | tf_op jit(solution)/shard_map/ppermute | solution.py:448
  28.7 3.1 %copy-start = (f32[512]{0:T(512)S(1)}, f32[512]{0:T(512)}, u32[]{:S(2)}) copy-start(f32[512]{0:T(512)} %param.16) | copy-start | bytes 6148
  28.7 3.1 %copy-start.1 = (f32[256]{0:T(256)S(1)}, f32[256]{0:T(256)}, u32[]{:S(2)}) copy-start(f32[256]{0:T(256)} %param.19) | copy-start | bytes 3076
  28.8 3.1 %collective-permute-start.12 = (f32[224,256]{1,0:T(8,128)S(1)}, f32[224,256]{1,0:T(8,128)S(1)}, u32[]{:S(2)}, u32[]{:S(2)}) collective-permute-start(f32[224,256]{1,0:T(8,128)S(1)} %get-tuple-element.33), channel_id=1, source_target_pairs={{0,1},{1,0},{2,3},{3,2},{4,5},{5,4},{6,7},{7,6},{8,9},{9,8},{10,11... | collective-permute-start | bytes 688136 | tf_op jit(solution)/shard_map/ppermute | solution.py:448
  30.4 1.5 %collective-permute-start.13 = (bf16[160,512]{1,0:T(8,128)(2,1)S(1)}, bf16[160,512]{1,0:T(8,128)(2,1)S(1)}, u32[]{:S(2)}, u32[]{:S(2)}) collective-permute-start(bf16[160,512]{1,0:T(8,128)(2,1)S(1)} %collective-permute-done.7.block_ref), channel_id=1, source_target_pairs={{0,1},{1,0},{2,3},{3,2},{4,5},{5,4},{6,7},{7,6},{8,9},{9,8},{10,11... | collective-permute-start | bytes 491528 | tf_op jit(solution)/shard_map/ppermute | solution.py:448

commit v2 on v1

--- a/solution.py
+++ b/solution.py
@@ -169,6 +169,7 @@
     row = lax.axis_index("rows")
     has_top, has_bottom = row > 0, row < lax.axis_size("rows") - 1
     fill = jnp.zeros((side_slots(height) - height - 2, channels), F32)
+    columns, ends = [], []
     for t in range(3):
         pair = []
         for k in range(2):
@@ -196,13 +197,16 @@
         tile = (frame_ref[...] if t == 2 else cache_ref[t]).astype(F32)
         column = jnp.where(odd == 0, tile[0], tile[width - 1])
         corners = [facing(odd == 0, v, lambda c: slice(c, c + 1)) for v in (top, bottom)]
-        cross_ref[t] = jnp.concatenate([column, *corners, fill], axis=0).astype(BF16)
+        columns.append(column)
+        ends += corners
+    cross_ref[...] = to_side(columns, ends)
 
 
 def pack_cols_kernel(frame_ref, cache_ref, top_ref, bottom_ref, twin_ref, cross_ref):
     width, height, channels = frame_ref.shape
     odd = lax.rem(lax.axis_index("cols"), 2)
     fill = jnp.zeros((side_slots(height) - height - 2, channels), F32)
+    columns, ends = [], []
     for t in range(3):
         sides = []
         for c in (0, width - 1):
@@ -212,7 +216,10 @@
             sides.append(jnp.concatenate([own, top, bottom, fill], axis=0))
         left, right = sides
         twin_ref[t] = jnp.where(odd == 1, left, right).astype(BF16)
-        cross_ref[t] = jnp.where(odd == 1, right, left).astype(BF16)
+        side = jnp.where(odd == 1, right, left)
+        columns.append(side[:height])
+        ends.append(side[height : height + 2])
+    cross_ref[...] = to_side(columns, [e[k : k + 1] for e in ends for k in range(2)])
 
 
 def extended(own, top, bottom, twin, cross, odd):
@@ -233,6 +240,19 @@
     return jnp.concatenate(
         [edge(top, height), left[:height], own, right[:height], edge(bottom, height + 1)], axis=0
     )
+
+
+def from_side(ref, t):
+    height = (ref.shape[0] - 8) // 3
+    side = ref[...].astype(F32)
+    fill = jnp.zeros((side_slots(height) - height - 2, side.shape[1]), F32)
+    at = 3 * height + 2 * t
+    return jnp.concatenate([side[t * height : (t + 1) * height], side[at : at + 2], fill], axis=0)
+
+
+def to_side(columns, corners):
+    fill = jnp.zeros((8 - len(corners), corners[0].shape[1]), F32)
+    return jnp.concatenate([*columns, *corners, fill], axis=0).astype(BF16)
 
 
 def tap_rows(tokens, height, count):
@@ -275,7 +295,7 @@
                 top_ref[t].astype(F32),
                 bottom_ref[t].astype(F32),
                 twin_ref[t].astype(F32),
-                cross_ref[t].astype(F32),
+                from_side(cross_ref, t),
                 odd,
             ),
             height,
@@ -302,7 +322,7 @@
         top_ref[2].astype(F32),
         bottom_ref[2].astype(F32),
         twin_ref[2].astype(F32),
-        cross_ref[2].astype(F32),
+        from_side(cross_ref, 2),
         odd,
     )
     raw_ref[...] = tokens.astype(BF16)
@@ -466,6 +486,7 @@
     far_tiles = (frame_far, cache_far, gain_far)
     edge = ((3, rows, channels), BF16)
     side = ((3, side_slots(height), channels), BF16)
+    packed = ((3 * height + 8, channels), BF16)
     keys = ((count, channels), BF16)
     sems = [pltpu.SemaphoreType.DMA((3,))]
     hops = (chips - 1) // 2
@@ -482,7 +503,7 @@
         (mine,) = call(split_kernel, [((6 * rows + 2 * height, channels), BF16)], (cache, arrived_a, arrived_b))
         theirs = moved(mine, twin_pairs)
         top, bottom, twin, to_cross = call(
-            sort_edges_kernel, [edge, edge, side, side], (frame, cache, partner, mine, theirs)
+            sort_edges_kernel, [edge, edge, side, packed], (frame, cache, partner, mine, theirs)
         )
     else:
         frame, cache, gain, first_rows, last_rows = call(
@@ -494,7 +515,7 @@
         chain_b = moved(chain_b, ring)
         top = moved(last_rows, down)
         bottom = moved(first_rows, up)
-        to_twin, to_cross = call(pack_cols_kernel, [side, side], (frame, cache, top, bottom))
+        to_twin, to_cross = call(pack_cols_kernel, [side, packed], (frame, cache, top, bottom))
         twin = moved(to_twin, twin_pairs)
     cross = moved(to_cross, cross_pairs)
     blocks = [frame, chain_a, chain_b]

time: 34.3 us -> 34.1 us (level)
  no operation moved by 1% of the time
where the time goes in v2:
time: 34.1 us; the launch traced here: 34 us
  starting transfers between devices  17.9 us (52%)
  Pallas kernels  8.61 us (25%)
  waiting for transfers between devices  6.63 us (19%)
  between operations  0.81 us (2%)
    ppermute x14, starting transfers between devices, moved(): return lax.ppermute(value, AXES, pairs)  17.9 us
    pallas_call x11, Pallas kernels, call(): pl.pallas_call(kernel, in_specs=[VM] * len(args) + [pl.BlockSpec(memory_s...  8.61 us
    ppermute x14, waiting for transfers between devices, moved(): return lax.ppermute(value, AXES, pairs)  6.63 us
  transfers between devices with their start and end apart: 14, of which 5 were waited for; matrix products, arithmetic and copies ran while one was open for 0% of the time, Pallas kernels for 14%

profile of v2, /device:TPU:0, one launch (start us, length us, event | category | flops | bytes accessed | tf_op | source)
XLA Modules:
  0.0 34.0 jit_solution(9803352703002055662)
XLA Ops:
  0.6 0.0 copy-start.2
  0.6 0.0 copy-start.3
  0.7 0.0 copy-start.4
  0.7 0.0 copy-start.5
  0.7 1.3 %shard_map.113 = (bf16[20,8,512]{2,1,0:T(8,128)(2,1)S(1)}, bf16[2,20,8,512]{3,2,1,0:T(8,128)(2,1)S(1)}, f32[1,512]{1,0:T(1,128)S(1)}, bf16[208,512]{1,0:T(8,128)(2,1)S(1)}, bf16[208,512]{1,0:T(8,128)(2,1)S(1)}) custom-call(bf16[20,8,512]{2,1,0:T(8,128)(2,1)} %bitcast.16, bf16[2,20,8,512]{3,2,1,0:T(8,128)(2,1)} %bitcast.15, f32[1,512]{1,0:T(1,128)} %bitcast.19), custom_call_target="tpu_custom_call" | custom-call | flops 2000000000 | bytes 4194304 | tf_op jit(solution)/shard_map/pallas_call | solution.py:25
  2.0 0.6 %collective-permute-start = (bf16[208,512]{1,0:T(8,128)(2,1)S(1)}, bf16[208,512]{1,0:T(8,128)(2,1)S(1)}, u32[]{:S(2)}, u32[]{:S(2)}) collective-permute-start(bf16[208,512]{1,0:T(8,128)(2,1)S(1)} %get-tuple-element.23), channel_id=1, source_target_pairs={{0,1},{1,0},{2,3},{3,2},{4,5},{5,4},{6,7},{7,6},{8,9},{9,8},{10,11... | collective-permute-start | bytes 638984 | tf_op jit(solution)/shard_map/ppermute | solution.py:468
  2.6 2.6 %collective-permute-start.1 = (bf16[208,512]{1,0:T(8,128)(2,1)S(1)}, bf16[208,512]{1,0:T(8,128)(2,1)S(1)}, u32[]{:S(2)}, u32[]{:S(2)}) collective-permute-start(bf16[208,512]{1,0:T(8,128)(2,1)S(1)} %get-tuple-element.24), channel_id=1, source_target_pairs={{4,8},{9,5},{8,12},{13,9},{12,14},{15,13},{14,10},{11,15},{10,6},{... | collective-permute-start | bytes 638984 | tf_op jit(solution)/shard_map/ppermute | solution.py:468
  5.2 0.0 collective-permute-done.partner_ref
  5.2 1.6 %collective-permute-start.2 = (bf16[208,512]{1,0:T(8,128)(2,1)S(1)}, bf16[208,512]{1,0:T(8,128)(2,1)S(1)}, u32[]{:S(2)}, u32[]{:S(2)}) collective-permute-start(bf16[208,512]{1,0:T(8,128)(2,1)S(1)} %collective-permute-done.partner_ref), channel_id=1, source_target_pairs={{4,8},{9,5},{8,12},{13,9},{12,14},{15,13},{14,10},{11,15},{10,6},{... | collective-permute-start | bytes 638984 | tf_op jit(solution)/shard_map/ppermute | solution.py:468
  6.8 0.0 copy-done.2
  6.8 0.0 copy-done.3
  6.8 0.0 copy-done.4
  6.8 0.0 copy-done.5
  6.8 0.7 %shard_map.116 = (bf16[512,512]{1,0:T(8,128)(2,1)S(1)}, bf16[512,512]{1,0:T(8,128)(2,1)S(1)}) custom-call(bf16[512,512]{1,0:T(8,128)(2,1)S(1)} %copy-done.2, bf16[512,512]{1,0:T(8,128)(2,1)S(1)} %copy-done.3, bf16[512,512]{1,0:T(8,128)(2,1)S(1)} %copy-done.4, bf16[512,512]{1,0:T(8,128)(2,1)S(1)} %copy-done.5), custom_call_target="tpu_custom_call" | custom-call | flops 2000000000 | bytes 4194304 | tf_op jit(solution)/shard_map/pallas_call | solution.py:25
  7.5 1.4 %collective-permute-done.1.a_ref.arrived_ref = bf16[208,512]{1,0:T(8,128)(2,1)S(1)} collective-permute-done((bf16[208,512]{1,0:T(8,128)(2,1)S(1)}, bf16[208,512]{1,0:T(8,128)(2,1)S(1)}, u32[]{:S(2)}, u32[]{:S(2)}) %collective-permute-start.1) | collective-permute-done | bytes 213024 | tf_op jit(solution)/shard_map/ppermute | solution.py:468
  8.9 2.3 %collective-permute-done.2.b_ref.arrived_ref = bf16[208,512]{1,0:T(8,128)(2,1)S(1)} collective-permute-done((bf16[208,512]{1,0:T(8,128)(2,1)S(1)}, bf16[208,512]{1,0:T(8,128)(2,1)S(1)}, u32[]{:S(2)}, u32[]{:S(2)}) %collective-permute-start.2) | collective-permute-done | bytes 213024 | tf_op jit(solution)/shard_map/ppermute | solution.py:468
  11.2 0.1 shard_map.114.mine_ref
  11.3 0.1 collective-permute-start.3
  11.4 2.2 %collective-permute-start.5 = (bf16[160,512]{1,0:T(8,128)(2,1)S(1)}, bf16[160,512]{1,0:T(8,128)(2,1)S(1)}, u32[]{:S(2)}, u32[]{:S(2)}) collective-permute-start(bf16[160,512]{1,0:T(8,128)(2,1)S(1)} %shard_map.118.refs_1_), channel_id=1, source_target_pairs={{4,8},{9,5},{8,12},{13,9},{12,14},{15,13},{14,10},{11,15},{10,6},{... | collective-permute-start | bytes 491528 | tf_op jit(solution)/shard_map/ppermute | solution.py:468
  13.6 0.0 collective-permute-done.3.theirs_ref
  13.6 0.1 shard_map.115
  13.7 0.7 %collective-permute-start.4 = (bf16[32,512]{1,0:T(8,128)(2,1)S(1)}, bf16[32,512]{1,0:T(8,128)(2,1)S(1)}, u32[]{:S(2)}, u32[]{:S(2)}) collective-permute-start(bf16[32,512]{1,0:T(8,128)(2,1)S(1)} %get-tuple-element.28), channel_id=1, source_target_pairs={{1,2},{2,1},{5,6},{6,5},{9,10},{10,9},{13,14},{14,13},{17,18},{18,... | collective-permute-start | bytes 98312 | tf_op jit(solution)/shard_map/ppermute | solution.py:468
  14.4 1.6 %collective-permute-start.9 = (bf16[160,512]{1,0:T(8,128)(2,1)S(1)}, bf16[160,512]{1,0:T(8,128)(2,1)S(1)}, u32[]{:S(2)}, u32[]{:S(2)}) collective-permute-start(bf16[160,512]{1,0:T(8,128)(2,1)S(1)} %shard_map.119.refs_2_), channel_id=1, source_target_pairs={{4,8},{9,5},{8,12},{13,9},{12,14},{15,13},{14,10},{11,15},{10,6},{... | collective-permute-start | bytes 491528 | tf_op jit(solution)/shard_map/ppermute | solution.py:468
  16.1 0.0 collective-permute-done.4.cross_ref
  16.1 0.0 slice-start
  16.1 0.0 slice-start.1
  16.1 0.4 %shard_map.117 = (bf16[224,512]{1,0:T(8,128)(2,1)S(1)}, bf16[224,512]{1,0:T(8,128)(2,1)S(1)}) custom-call(bf16[20,8,512]{2,1,0:T(8,128)(2,1)S(1)} %get-tuple-element.21.frame_ref.refs_0_, bf16[3,24,512]{2,1,0:T(8,128)(2,1)S(1)} %get-tuple-element.25.top_ref, bf16[3,24,512]{2,1,0:T(8,128)(2,1)S(1)} %get-tuple-element.26.bottom_ref, ...), custom_call_target="tpu_custom_call" | custom-call | flops 2000000000 | bytes 4194304 | tf_op jit(solution)/shard_map/pallas_call | solution.py:25
  16.4 3.1 %collective-permute-start.8 = (bf16[224,512]{1,0:T(8,128)(2,1)S(1)}, bf16[224,512]{1,0:T(8,128)(2,1)S(1)}, u32[]{:S(2)}, u32[]{:S(2)}) collective-permute-start(bf16[224,512]{1,0:T(8,128)(2,1)S(1)} %get-tuple-element.30.own_ref.query_ref), channel_id=1, source_target_pairs={{0,1},{1,0},{2,3},{3,2},{4,5},{5,4},{6,7},{7,6},{8,9},{9,8},{10,11... | collective-permute-start | bytes 688136 | tf_op jit(solution)/shard_map/ppermute | solution.py:468
  19.5 0.0 collective-permute-done.5.refs_3_
  19.5 1.6 %collective-permute-start.6 = (bf16[160,512]{1,0:T(8,128)(2,1)S(1)}, bf16[160,512]{1,0:T(8,128)(2,1)S(1)}, u32[]{:S(2)}, u32[]{:S(2)}) collective-permute-start(bf16[160,512]{1,0:T(8,128)(2,1)S(1)} %collective-permute-done.5.refs_3_), channel_id=1, source_target_pairs={{4,8},{9,5},{8,12},{13,9},{12,14},{15,13},{14,10},{11,15},{10,6},{... | collective-permute-start | bytes 491528 | tf_op jit(solution)/shard_map/ppermute | solution.py:468
  21.2 0.0 collective-permute-done.9.refs_4_
  21.2 1.6 %collective-permute-start.10 = (bf16[160,512]{1,0:T(8,128)(2,1)S(1)}, bf16[160,512]{1,0:T(8,128)(2,1)S(1)}, u32[]{:S(2)}, u32[]{:S(2)}) collective-permute-start(bf16[160,512]{1,0:T(8,128)(2,1)S(1)} %collective-permute-done.9.refs_4_), channel_id=1, source_target_pairs={{4,8},{9,5},{8,12},{13,9},{12,14},{15,13},{14,10},{11,15},{10,6},{... | collective-permute-start | bytes 491528 | tf_op jit(solution)/shard_map/ppermute | solution.py:468
  22.7 2.1 %collective-permute-done.6.refs_5_ = bf16[160,512]{1,0:T(8,128)(2,1)S(1)} collective-permute-done((bf16[160,512]{1,0:T(8,128)(2,1)S(1)}, bf16[160,512]{1,0:T(8,128)(2,1)S(1)}, u32[]{:S(2)}, u32[]{:S(2)}) %collective-permute-start.6) | collective-permute-done | bytes 163872 | tf_op jit(solution)/shard_map/ppermute | solution.py:468
  24.9 1.6 %collective-permute-start.7 = (bf16[160,512]{1,0:T(8,128)(2,1)S(1)}, bf16[160,512]{1,0:T(8,128)(2,1)S(1)}, u32[]{:S(2)}, u32[]{:S(2)}) collective-permute-start(bf16[160,512]{1,0:T(8,128)(2,1)S(1)} %collective-permute-done.6.refs_5_), channel_id=1, source_target_pairs={{4,8},{9,5},{8,12},{13,9},{12,14},{15,13},{14,10},{11,15},{10,6},{... | collective-permute-start | bytes 491528 | tf_op jit(solution)/shard_map/ppermute | solution.py:468
  26.5 0.1 collective-permute-done.10.refs_6_
  26.6 0.0 collective-permute-done.8.twin_ref
  26.6 1.9 %shard_map.120 = (f32[224,768]{1,0:T(8,128)S(1)}, bf16[224,512]{1,0:T(8,128)(2,1)S(1)}, f32[224,256]{1,0:T(8,128)S(1)}) custom-call(f32[1,512]{1,0:T(1,128)S(1)} %get-tuple-element.20.gain_ref.key_gain_ref, bf16[224,512]{1,0:T(8,128)(2,1)S(1)} %get-tuple-element.30.own_ref.query_ref, bf16[224,512]{1,0:T(8,128)(2,1)S(1)} %collective-permute-done.8.twin_ref, ...), custom_call_target="tpu_custom_call" | custom-call | flops 2000000000 | bytes 4194304 | tf_op jit(solution)/shard_map/pallas_call | solution.py:25
  28.5 0.1 collective-permute-start.11
  28.6 0.0 copy-start
  28.6 0.0 copy-start.1
  28.6 0.5 %collective-permute-start.12 = (f32[224,256]{1,0:T(8,128)S(1)}, f32[224,256]{1,0:T(8,128)S(1)}, u32[]{:S(2)}, u32[]{:S(2)}) collective-permute-start(f32[224,256]{1,0:T(8,128)S(1)} %get-tuple-element.33), channel_id=1, source_target_pairs={{0,1},{1,0},{2,3},{3,2},{4,5},{5,4},{6,7},{7,6},{8,9},{9,8},{10,11... | collective-permute-start | bytes 688136 | tf_op jit(solution)/shard_map/ppermute | solution.py:468
  29.1 0.0 slice-done
  29.1 0.0 slice-done.1
  29.1 1.1 %shard_map.122.partial_ref = f32[160,256]{1,0:T(8,128)S(1)} custom-call(bf16[2,20,8,512]{3,2,1,0:T(8,128)(2,1)S(1)} %get-tuple-element.22.cache_ref, bf16[3,24,512]{2,1,0:T(8,128)(2,1)S(1)} %get-tuple-element.25.top_ref, bf16[3,24,512]{2,1,0:T(8,128)(2,1)S(1)} %get-tuple-element.26.bottom_ref, bf16[3,16,512]{2,1,0:T(8,128)(2,1)S(1)} %get-tuple-element.27.twin_ref, ...), custom_call_target="tpu_custom_call" | custom-call | flops 2000000000 | bytes 4194304 | tf_op jit(solution)/shard_map/pallas_call | solution.py:25
  30.2 0.0 collective-permute-done.7.block_ref
  30.2 0.2 collective-permute-start.13
  30.3 0.6 %shard_map.121.state_ref = f32[224,768]{1,0:T(8,128)S(1)} custom-call(f32[1,512]{1,0:T(1,128)S(1)} %get-tuple-element.20.gain_ref.key_gain_ref, bf16[224,512]{1,0:T(8,128)(2,1)S(1)} %get-tuple-element.30.own_ref.query_ref, bf16[160,512]{1,0:T(8,128)(2,1)S(1)} %collective-permute-done.7.block_ref, f32[224,768]{1,0:T(8,128)S(1)} %get-tuple-element.31.state_ref), custom_call_target="tpu_custom_call" | custom-call | flops 2000000000 | bytes 4194304 | tf_op jit(solution)/shard_map/pallas_call | solution.py:25
  31.0 0.7 %collective-permute-done.13.last_ref = bf16[160,512]{1,0:T(8,128)(2,1)S(1)} collective-permute-done((bf16[160,512]{1,0:T(8,128)(2,1)S(1)}, bf16[160,512]{1,0:T(8,128)(2,1)S(1)}, u32[]{:S(2)}, u32[]{:S(2)}) %collective-permute-start.13) | collective-permute-done | bytes 163872 | tf_op jit(solution)/shard_map/ppermute | solution.py:468
  31.6 0.0 collective-permute-done.11.other_ref
  31.6 0.0 collective-permute-done.12.scale_ref
  31.7 0.0 copy-done
  31.7 0.0 copy-done.1
  31.7 2.3 %shard_map.123 = (bf16[160,512]{1,0:T(8,128)(2,1)}, bf16[160,256]{1,0:T(8,128)(2,1)}) custom-call(f32[224,768]{1,0:T(8,128)S(1)} %shard_map.121.state_ref, bf16[224,512]{1,0:T(8,128)(2,1)S(1)} %collective-permute-done.11.other_ref, f32[224,256]{1,0:T(8,128)S(1)} %collective-permute-done.12.scale_ref, ...), custom_call_target="tpu_custom_call" | custom-call | flops 2000000000 | bytes 4194304 | tf_op jit(solution)/shard_map/pallas_call | solution.py:25
  (3 shorter events, 0.0 us)
Async XLA Ops:
  0.6 6.2 %copy-start.2 = (bf16[512,512]{1,0:T(8,128)(2,1)S(1)}, bf16[512,512]{1,0:T(8,128)(2,1)}, u32[]{:S(2)}) copy-start(bf16[512,512]{1,0:T(8,128)(2,1)} %wq_ref.1) | copy-start | bytes 1572868
  0.6 6.1 %copy-start.3 = (bf16[512,512]{1,0:T(8,128)(2,1)S(1)}, bf16[512,512]{1,0:T(8,128)(2,1)}, u32[]{:S(2)}) copy-start(bf16[512,512]{1,0:T(8,128)(2,1)} %wk_ref.1) | copy-start | bytes 1572868
  0.7 6.1 %copy-start.4 = (bf16[512,512]{1,0:T(8,128)(2,1)S(1)}, bf16[512,512]{1,0:T(8,128)(2,1)}, u32[]{:S(2)}) copy-start(bf16[512,512]{1,0:T(8,128)(2,1)} %wv_ref.1) | copy-start | bytes 1572868
  0.7 6.1 %copy-start.5 = (bf16[512,512]{1,0:T(8,128)(2,1)S(1)}, bf16[512,512]{1,0:T(8,128)(2,1)}, u32[]{:S(2)}) copy-start(bf16[512,512]{1,0:T(8,128)(2,1)} %wo_ref.1) | copy-start | bytes 1572868
  2.0 3.2 %collective-permute-start = (bf16[208,512]{1,0:T(8,128)(2,1)S(1)}, bf16[208,512]{1,0:T(8,128)(2,1)S(1)}, u32[]{:S(2)}, u32[]{:S(2)}) collective-permute-start(bf16[208,512]{1,0:T(8,128)(2,1)S(1)} %get-tuple-element.23), channel_id=1, source_target_pairs={{0,1},{1,0},{2,3},{3,2},{4,5},{5,4},{6,7},{7,6},{8,9},{9,8},{10,11... | collective-permute-start | bytes 638984 | tf_op jit(solution)/shard_map/ppermute | solution.py:468
  2.6 6.4 %collective-permute-start.1 = (bf16[208,512]{1,0:T(8,128)(2,1)S(1)}, bf16[208,512]{1,0:T(8,128)(2,1)S(1)}, u32[]{:S(2)}, u32[]{:S(2)}) collective-permute-start(bf16[208,512]{1,0:T(8,128)(2,1)S(1)} %get-tuple-element.24), channel_id=1, source_target_pairs={{4,8},{9,5},{8,12},{13,9},{12,14},{15,13},{14,10},{11,15},{10,6},{... | collective-permute-start | bytes 638984 | tf_op jit(solution)/shard_map/ppermute | solution.py:468
  5.2 6.0 %collective-permute-start.2 = (bf16[208,512]{1,0:T(8,128)(2,1)S(1)}, bf16[208,512]{1,0:T(8,128)(2,1)S(1)}, u32[]{:S(2)}, u32[]{:S(2)}) collective-permute-start(bf16[208,512]{1,0:T(8,128)(2,1)S(1)} %collective-permute-done.partner_ref), channel_id=1, source_target_pairs={{4,8},{9,5},{8,12},{13,9},{12,14},{15,13},{14,10},{11,15},{10,6},{... | collective-permute-start | bytes 638984 | tf_op jit(solution)/shard_map/ppermute | solution.py:468
  11.3 2.3 %collective-permute-start.3 = (bf16[160,512]{1,0:T(8,128)(2,1)S(1)}, bf16[160,512]{1,0:T(8,128)(2,1)S(1)}, u32[]{:S(2)}, u32[]{:S(2)}) collective-permute-start(bf16[160,512]{1,0:T(8,128)(2,1)S(1)} %shard_map.114.mine_ref), channel_id=1, source_target_pairs={{0,1},{1,0},{2,3},{3,2},{4,5},{5,4},{6,7},{7,6},{8,9},{9,8},{10,11... | collective-permute-start | bytes 491528 | tf_op jit(solution)/shard_map/ppermute | solution.py:468
  11.4 8.1 %collective-permute-start.5 = (bf16[160,512]{1,0:T(8,128)(2,1)S(1)}, bf16[160,512]{1,0:T(8,128)(2,1)S(1)}, u32[]{:S(2)}, u32[]{:S(2)}) collective-permute-start(bf16[160,512]{1,0:T(8,128)(2,1)S(1)} %shard_map.118.refs_1_), channel_id=1, source_target_pairs={{4,8},{9,5},{8,12},{13,9},{12,14},{15,13},{14,10},{11,15},{10,6},{... | collective-permute-start | bytes 491528 | tf_op jit(solution)/shard_map/ppermute | solution.py:468
  13.7 2.3 %collective-permute-start.4 = (bf16[32,512]{1,0:T(8,128)(2,1)S(1)}, bf16[32,512]{1,0:T(8,128)(2,1)S(1)}, u32[]{:S(2)}, u32[]{:S(2)}) collective-permute-start(bf16[32,512]{1,0:T(8,128)(2,1)S(1)} %get-tuple-element.28), channel_id=1, source_target_pairs={{1,2},{2,1},{5,6},{6,5},{9,10},{10,9},{13,14},{14,13},{17,18},{18,... | collective-permute-start | bytes 98312 | tf_op jit(solution)/shard_map/ppermute | solution.py:468
  14.4 6.7 %collective-permute-start.9 = (bf16[160,512]{1,0:T(8,128)(2,1)S(1)}, bf16[160,512]{1,0:T(8,128)(2,1)S(1)}, u32[]{:S(2)}, u32[]{:S(2)}) collective-permute-start(bf16[160,512]{1,0:T(8,128)(2,1)S(1)} %shard_map.119.refs_2_), channel_id=1, source_target_pairs={{4,8},{9,5},{8,12},{13,9},{12,14},{15,13},{14,10},{11,15},{10,6},{... | collective-permute-start | bytes 491528 | tf_op jit(solution)/shard_map/ppermute | solution.py:468
  16.1 13.0 %slice-start = ((s8[7077888]{0:T(1024)(128)(4,1)}), s8[4194304]{0:T(1024)(128)(4,1)S(1)}, s32[]{:S(2)}) async-start(s8[7077888]{0:T(1024)(128)(4,1)} %bitcast.11), calls=%async_computation | async-start | bytes 8388608
  16.1 13.0 %slice-start.1 = ((s8[7077888]{0:T(1024)(128)(4,1)}), s8[2883584]{0:T(1024)(128)(4,1)S(1)}, s32[]{:S(2)}) async-start(s8[7077888]{0:T(1024)(128)(4,1)} %bitcast.11), calls=%async_computation.1 | async-start | bytes 5767168
  16.4 10.2 %collective-permute-start.8 = (bf16[224,512]{1,0:T(8,128)(2,1)S(1)}, bf16[224,512]{1,0:T(8,128)(2,1)S(1)}, u32[]{:S(2)}, u32[]{:S(2)}) collective-permute-start(bf16[224,512]{1,0:T(8,128)(2,1)S(1)} %get-tuple-element.30.own_ref.query_ref), channel_id=1, source_target_pairs={{0,1},{1,0},{2,3},{3,2},{4,5},{5,4},{6,7},{7,6},{8,9},{9,8},{10,11... | collective-permute-start | bytes 688136 | tf_op jit(solution)/shard_map/ppermute | solution.py:468
  19.5 5.3 %collective-permute-start.6 = (bf16[160,512]{1,0:T(8,128)(2,1)S(1)}, bf16[160,512]{1,0:T(8,128)(2,1)S(1)}, u32[]{:S(2)}, u32[]{:S(2)}) collective-permute-start(bf16[160,512]{1,0:T(8,128)(2,1)S(1)} %collective-permute-done.5.refs_3_), channel_id=1, source_target_pairs={{4,8},{9,5},{8,12},{13,9},{12,14},{15,13},{14,10},{11,15},{10,6},{... | collective-permute-start | bytes 491528 | tf_op jit(solution)/shard_map/ppermute | solution.py:468
  21.2 5.5 %collective-permute-start.10 = (bf16[160,512]{1,0:T(8,128)(2,1)S(1)}, bf16[160,512]{1,0:T(8,128)(2,1)S(1)}, u32[]{:S(2)}, u32[]{:S(2)}) collective-permute-start(bf16[160,512]{1,0:T(8,128)(2,1)S(1)} %collective-permute-done.9.refs_4_), channel_id=1, source_target_pairs={{4,8},{9,5},{8,12},{13,9},{12,14},{15,13},{14,10},{11,15},{10,6},{... | collective-permute-start | bytes 491528 | tf_op jit(solution)/shard_map/ppermute | solution.py:468
  24.9 5.3 %collective-permute-start.7 = (bf16[160,512]{1,0:T(8,128)(2,1)S(1)}, bf16[160,512]{1,0:T(8,128)(2,1)S(1)}, u32[]{:S(2)}, u32[]{:S(2)}) collective-permute-start(bf16[160,512]{1,0:T(8,128)(2,1)S(1)} %collective-permute-done.6.refs_5_), channel_id=1, source_target_pairs={{4,8},{9,5},{8,12},{13,9},{12,14},{15,13},{14,10},{11,15},{10,6},{... | collective-permute-start | bytes 491528 | tf_op jit(solution)/shard_map/ppermute | solution.py:468
  28.5 3.2 %collective-permute-start.11 = (bf16[224,512]{1,0:T(8,128)(2,1)S(1)}, bf16[224,512]{1,0:T(8,128)(2,1)S(1)}, u32[]{:S(2)}, u32[]{:S(2)}) collective-permute-start(bf16[224,512]{1,0:T(8,128)(2,1)S(1)} %get-tuple-element.32), channel_id=1, source_target_pairs={{0,1},{1,0},{2,3},{3,2},{4,5},{5,4},{6,7},{7,6},{8,9},{9,8},{10,11... | collective-permute-start | bytes 688136 | tf_op jit(solution)/shard_map/ppermute | solution.py:468
  28.6 3.1 %copy-start = (f32[512]{0:T(512)S(1)}, f32[512]{0:T(512)}, u32[]{:S(2)}) copy-start(f32[512]{0:T(512)} %param.16) | copy-start | bytes 6148
  28.6 3.1 %copy-start.1 = (f32[256]{0:T(256)S(1)}, f32[256]{0:T(256)}, u32[]{:S(2)}) copy-start(f32[256]{0:T(256)} %param.19) | copy-start | bytes 3076
  28.6 3.1 %collective-permute-start.12 = (f32[224,256]{1,0:T(8,128)S(1)}, f32[224,256]{1,0:T(8,128)S(1)}, u32[]{:S(2)}, u32[]{:S(2)}) collective-permute-start(f32[224,256]{1,0:T(8,128)S(1)} %get-tuple-element.33), channel_id=1, source_target_pairs={{0,1},{1,0},{2,3},{3,2},{4,5},{5,4},{6,7},{7,6},{8,9},{9,8},{10,11... | collective-permute-start | bytes 688136 | tf_op jit(solution)/shard_map/ppermute | solution.py:468
  30.2 1.5 %collective-permute-start.13 = (bf16[160,512]{1,0:T(8,128)(2,1)S(1)}, bf16[160,512]{1,0:T(8,128)(2,1)S(1)}, u32[]{:S(2)}, u32[]{:S(2)}) collective-permute-start(bf16[160,512]{1,0:T(8,128)(2,1)S(1)} %collective-permute-done.7.block_ref), channel_id=1, source_target_pairs={{0,1},{1,0},{2,3},{3,2},{4,5},{5,4},{6,7},{7,6},{8,9},{9,8},{10,11... | collective-permute-start | bytes 491528 | tf_op jit(solution)/shard_map/ppermute | solution.py:468

commit v3 on v2

--- a/solution.py
+++ b/solution.py
@@ -334,15 +334,19 @@
     return jnp.broadcast_to(value, (value.shape[0], width))
 
 
-def key_rows(refs, gain):
-    parts = [
+def key_rows(refs, gain, ready=()):
+    parts = [ref[...] for ref in ready] + [
         rms_scaled(ref[...].reshape(-1, gain.shape[1]).astype(F32), gain).astype(BF16) for ref in refs
     ]
     return parts[0] if len(parts) == 1 else jnp.concatenate(parts, axis=0)
 
 
-def fold_kernel(blocks, first, last, gain_ref, own_ref, twin_ref, *refs):
-    keys = key_rows(refs[:blocks], gain_ref[...])
+def norm_kernel(gain_ref, *refs):
+    refs[-1][...] = key_rows(refs[:-1], gain_ref[...])
+
+
+def fold_kernel(blocks, ready, first, last, gain_ref, own_ref, twin_ref, *refs):
+    keys = key_rows(refs[ready:blocks], gain_ref[...], refs[:ready])
     refs = refs[blocks:]
     states, outs = ((None, None), refs) if first else (refs[:2], refs[2:])
     channels = keys.shape[1]
@@ -375,12 +379,12 @@
             out[:, channels + 128 :] = lanes(total, 128)
 
 
-def fold(states, own, twin, gain, blocks, last):
+def fold(states, own, twin, gain, blocks, ready, last):
     length, channels = own.shape
     shape = ((length, channels + 256), F32)
     first = states is None
     args = (gain, own, twin, *blocks, *(() if first else states))
-    kernel = functools.partial(fold_kernel, len(blocks), first, last)
+    kernel = functools.partial(fold_kernel, len(blocks), ready, first, last)
     others = [((length, channels), BF16), ((length, 256), F32)] if last else [shape]
     return call(kernel, [shape, *others], args, 24 << 20)
 
@@ -538,8 +542,14 @@
     twin_queries = moved(queries, twin_pairs)
     (partial,) = call(cache_conv_kernel, [((count, out_channels), F32)], (cache, top, bottom, twin, cross, w_conv))
     states = None
+    ready = 0
+    if len(blocks) <= 7:
+        early = blocks[:-2]
+        shape = ((len(early) * count, channels), BF16)
+        blocks = [*call(norm_kernel, [shape], (gain, *early)), *blocks[-2:]]
+        ready = 1
     for k in range(0, len(blocks), 7):
-        states = fold(states, queries, twin_queries, gain, blocks[k : k + 7], k + 7 >= len(blocks))
+        states = fold(states, queries, twin_queries, gain, blocks[k : k + 7], ready, k + 7 >= len(blocks))
     other = moved(states[1], twin_pairs)
     other_scale = moved(states[2], twin_pairs)
     (state,) = call(fold_own_kernel, [(states[0].shape, F32)], (gain, queries, last_a, states[0]))

time: 34.1 us -> 35.2 us (1.032)
  waiting for transfers between devices: 6.63 us -> 8.53 us
  starting transfers between devices: 17.9 us -> 17 us
    ppermute x14, waiting for transfers between devices: 6.63 us -> 8.53 us  [moved(): return lax.ppermute(value, AXES, pairs)]
    ppermute x14, starting transfers between devices: 17.9 us -> 17 us  [moved(): return lax.ppermute(value, AXES, pairs)]
    pallas_call x11 -> x12, Pallas kernels: 8.61 us -> 8.63 us  [call(): pl.pallas_call(kernel, in_specs=[VM] * len(args) + [pl.BlockSpec(memory_s...]
  transfers between devices with their start and end apart: 14 -> 14, of which waited for: 5 -> 5; matrix products, arithmetic and copies ran while one was open for 0% -> 0% of each run, Pallas kernels for 14% -> 15%
where the time goes in v3:
time: 35.2 us; the launch traced here: 35 us
  starting transfers between devices  17 us (48%)
  Pallas kernels  8.63 us (25%)
  waiting for transfers between devices  8.53 us (24%)
  between operations  0.81 us (2%)
    ppermute x14, starting transfers between devices, moved(): return lax.ppermute(value, AXES, pairs)  17 us
    pallas_call x12, Pallas kernels, call(): pl.pallas_call(kernel, in_specs=[VM] * len(args) + [pl.BlockSpec(memory_s...  8.63 us
    ppermute x14, waiting for transfers between devices, moved(): return lax.ppermute(value, AXES, pairs)  8.53 us
  transfers between devices with their start and end apart: 14, of which 5 were waited for; matrix products, arithmetic and copies ran while one was open for 0% of the time, Pallas kernels for 15%

profile of v3, /device:TPU:0, one launch (start us, length us, event | category | flops | bytes accessed | tf_op | source)
XLA Modules:
  0.0 35.0 jit_solution(2063057362619880429)
XLA Ops:
  0.6 1.2 %shard_map.113 = (bf16[20,8,512]{2,1,0:T(8,128)(2,1)S(1)}, bf16[2,20,8,512]{3,2,1,0:T(8,128)(2,1)S(1)}, f32[1,512]{1,0:T(1,128)S(1)}, bf16[208,512]{1,0:T(8,128)(2,1)S(1)}, bf16[208,512]{1,0:T(8,128)(2,1)S(1)}) custom-call(bf16[20,8,512]{2,1,0:T(8,128)(2,1)} %bitcast.16, bf16[2,20,8,512]{3,2,1,0:T(8,128)(2,1)} %bitcast.15, f32[1,512]{1,0:T(1,128)} %bitcast.19), custom_call_target="tpu_custom_call" | custom-call | flops 2000000000 | bytes 4194304 | tf_op jit(solution)/shard_map/pallas_call | solution.py:25
  1.8 0.6 %collective-permute-start = (bf16[208,512]{1,0:T(8,128)(2,1)S(1)}, bf16[208,512]{1,0:T(8,128)(2,1)S(1)}, u32[]{:S(2)}, u32[]{:S(2)}) collective-permute-start(bf16[208,512]{1,0:T(8,128)(2,1)S(1)} %get-tuple-element.23), channel_id=1, source_target_pairs={{0,1},{1,0},{2,3},{3,2},{4,5},{5,4},{6,7},{7,6},{8,9},{9,8},{10,11... | collective-permute-start | bytes 638984 | tf_op jit(solution)/shard_map/ppermute | solution.py:472
  2.4 0.0 copy-start.2
  2.4 0.0 copy-start.3
  2.4 0.0 copy-start.4
  2.4 0.0 copy-start.5
  2.4 2.7 %collective-permute-start.1 = (bf16[208,512]{1,0:T(8,128)(2,1)S(1)}, bf16[208,512]{1,0:T(8,128)(2,1)S(1)}, u32[]{:S(2)}, u32[]{:S(2)}) collective-permute-start(bf16[208,512]{1,0:T(8,128)(2,1)S(1)} %get-tuple-element.24), channel_id=1, source_target_pairs={{4,8},{9,5},{8,12},{13,9},{12,14},{15,13},{14,10},{11,15},{10,6},{... | collective-permute-start | bytes 638984 | tf_op jit(solution)/shard_map/ppermute | solution.py:472
  5.1 0.0 collective-permute-done.partner_ref
  5.1 1.6 %collective-permute-start.2 = (bf16[208,512]{1,0:T(8,128)(2,1)S(1)}, bf16[208,512]{1,0:T(8,128)(2,1)S(1)}, u32[]{:S(2)}, u32[]{:S(2)}) collective-permute-start(bf16[208,512]{1,0:T(8,128)(2,1)S(1)} %collective-permute-done.partner_ref), channel_id=1, source_target_pairs={{4,8},{9,5},{8,12},{13,9},{12,14},{15,13},{14,10},{11,15},{10,6},{... | collective-permute-start | bytes 638984 | tf_op jit(solution)/shard_map/ppermute | solution.py:472
  6.7 2.2 %collective-permute-done.1.a_ref.arrived_ref = bf16[208,512]{1,0:T(8,128)(2,1)S(1)} collective-permute-done((bf16[208,512]{1,0:T(8,128)(2,1)S(1)}, bf16[208,512]{1,0:T(8,128)(2,1)S(1)}, u32[]{:S(2)}, u32[]{:S(2)}) %collective-permute-start.1) | collective-permute-done | bytes 213024 | tf_op jit(solution)/shard_map/ppermute | solution.py:472
  8.8 2.2 %collective-permute-start.5 = (bf16[160,512]{1,0:T(8,128)(2,1)S(1)}, bf16[160,512]{1,0:T(8,128)(2,1)S(1)}, u32[]{:S(2)}, u32[]{:S(2)}) collective-permute-start(bf16[160,512]{1,0:T(8,128)(2,1)S(1)} %shard_map.118.refs_1_), channel_id=1, source_target_pairs={{4,8},{9,5},{8,12},{13,9},{12,14},{15,13},{14,10},{11,15},{10,6},{... | collective-permute-start | bytes 491528 | tf_op jit(solution)/shard_map/ppermute | solution.py:472
  11.0 0.1 collective-permute-done.2.b_ref.arrived_ref
  11.1 0.1 shard_map.114.mine_ref
  11.2 0.1 collective-permute-start.3
  11.3 0.0 copy-done.2
  11.3 0.0 copy-done.3
  11.3 0.0 copy-done.4
  11.3 0.0 copy-done.5
  11.3 0.7 %shard_map.116 = (bf16[512,512]{1,0:T(8,128)(2,1)S(1)}, bf16[512,512]{1,0:T(8,128)(2,1)S(1)}) custom-call(bf16[512,512]{1,0:T(8,128)(2,1)S(1)} %copy-done.2, bf16[512,512]{1,0:T(8,128)(2,1)S(1)} %copy-done.3, bf16[512,512]{1,0:T(8,128)(2,1)S(1)} %copy-done.4, bf16[512,512]{1,0:T(8,128)(2,1)S(1)} %copy-done.5), custom_call_target="tpu_custom_call" | custom-call | flops 2000000000 | bytes 4194304 | tf_op jit(solution)/shard_map/pallas_call | solution.py:25
  12.1 2.1 %collective-permute-done.5.refs_3_ = bf16[160,512]{1,0:T(8,128)(2,1)S(1)} collective-permute-done((bf16[160,512]{1,0:T(8,128)(2,1)S(1)}, bf16[160,512]{1,0:T(8,128)(2,1)S(1)}, u32[]{:S(2)}, u32[]{:S(2)}) %collective-permute-start.5) | collective-permute-done | bytes 163872 | tf_op jit(solution)/shard_map/ppermute | solution.py:472
  14.2 2.1 %collective-permute-start.6 = (bf16[160,512]{1,0:T(8,128)(2,1)S(1)}, bf16[160,512]{1,0:T(8,128)(2,1)S(1)}, u32[]{:S(2)}, u32[]{:S(2)}) collective-permute-start(bf16[160,512]{1,0:T(8,128)(2,1)S(1)} %collective-permute-done.5.refs_3_), channel_id=1, source_target_pairs={{4,8},{9,5},{8,12},{13,9},{12,14},{15,13},{14,10},{11,15},{10,6},{... | collective-permute-start | bytes 491528 | tf_op jit(solution)/shard_map/ppermute | solution.py:472
  16.3 0.0 collective-permute-done.3.theirs_ref
  16.3 0.1 shard_map.115
  16.4 0.7 %collective-permute-start.4 = (bf16[32,512]{1,0:T(8,128)(2,1)S(1)}, bf16[32,512]{1,0:T(8,128)(2,1)S(1)}, u32[]{:S(2)}, u32[]{:S(2)}) collective-permute-start(bf16[32,512]{1,0:T(8,128)(2,1)S(1)} %get-tuple-element.28), channel_id=1, source_target_pairs={{1,2},{2,1},{5,6},{6,5},{9,10},{10,9},{13,14},{14,13},{17,18},{18,... | collective-permute-start | bytes 98312 | tf_op jit(solution)/shard_map/ppermute | solution.py:472
  17.1 1.6 %collective-permute-start.9 = (bf16[160,512]{1,0:T(8,128)(2,1)S(1)}, bf16[160,512]{1,0:T(8,128)(2,1)S(1)}, u32[]{:S(2)}, u32[]{:S(2)}) collective-permute-start(bf16[160,512]{1,0:T(8,128)(2,1)S(1)} %shard_map.119.refs_2_), channel_id=1, source_target_pairs={{4,8},{9,5},{8,12},{13,9},{12,14},{15,13},{14,10},{11,15},{10,6},{... | collective-permute-start | bytes 491528 | tf_op jit(solution)/shard_map/ppermute | solution.py:472
  18.8 0.0 collective-permute-done.4.cross_ref
  18.8 0.0 slice-start
  18.8 0.4 %shard_map.117 = (bf16[224,512]{1,0:T(8,128)(2,1)S(1)}, bf16[224,512]{1,0:T(8,128)(2,1)S(1)}) custom-call(bf16[20,8,512]{2,1,0:T(8,128)(2,1)S(1)} %get-tuple-element.21.frame_ref.refs_0_, bf16[3,24,512]{2,1,0:T(8,128)(2,1)S(1)} %get-tuple-element.25.top_ref, bf16[3,24,512]{2,1,0:T(8,128)(2,1)S(1)} %get-tuple-element.26.bottom_ref, ...), custom_call_target="tpu_custom_call" | custom-call | flops 2000000000 | bytes 4194304 | tf_op jit(solution)/shard_map/pallas_call | solution.py:25
  19.1 0.0 slice-start.1
  19.1 1.4 %collective-permute-start.8 = (bf16[224,512]{1,0:T(8,128)(2,1)S(1)}, bf16[224,512]{1,0:T(8,128)(2,1)S(1)}, u32[]{:S(2)}, u32[]{:S(2)}) collective-permute-start(bf16[224,512]{1,0:T(8,128)(2,1)S(1)} %get-tuple-element.30.own_ref.query_ref), channel_id=1, source_target_pairs={{0,1},{1,0},{2,3},{3,2},{4,5},{5,4},{6,7},{7,6},{8,9},{9,8},{10,11... | collective-permute-start | bytes 688136 | tf_op jit(solution)/shard_map/ppermute | solution.py:472
  20.5 0.0 collective-permute-done.6.refs_1_
  20.5 1.9 %collective-permute-start.7 = (bf16[160,512]{1,0:T(8,128)(2,1)S(1)}, bf16[160,512]{1,0:T(8,128)(2,1)S(1)}, u32[]{:S(2)}, u32[]{:S(2)}) collective-permute-start(bf16[160,512]{1,0:T(8,128)(2,1)S(1)} %collective-permute-done.6.refs_1_), channel_id=1, source_target_pairs={{4,8},{9,5},{8,12},{13,9},{12,14},{15,13},{14,10},{11,15},{10,6},{... | collective-permute-start | bytes 491528 | tf_op jit(solution)/shard_map/ppermute | solution.py:472
  22.4 0.0 collective-permute-done.9.refs_4_
  22.5 1.6 %collective-permute-start.10 = (bf16[160,512]{1,0:T(8,128)(2,1)S(1)}, bf16[160,512]{1,0:T(8,128)(2,1)S(1)}, u32[]{:S(2)}, u32[]{:S(2)}) collective-permute-start(bf16[160,512]{1,0:T(8,128)(2,1)S(1)} %collective-permute-done.9.refs_4_), channel_id=1, source_target_pairs={{4,8},{9,5},{8,12},{13,9},{12,14},{15,13},{14,10},{11,15},{10,6},{... | collective-permute-start | bytes 491528 | tf_op jit(solution)/shard_map/ppermute | solution.py:472
  24.1 0.3 shard_map.120.refs_0_
  24.4 3.4 %collective-permute-done.10.refs_2_ = bf16[160,512]{1,0:T(8,128)(2,1)S(1)} collective-permute-done((bf16[160,512]{1,0:T(8,128)(2,1)S(1)}, bf16[160,512]{1,0:T(8,128)(2,1)S(1)}, u32[]{:S(2)}, u32[]{:S(2)}) %collective-permute-start.10) | collective-permute-done | bytes 163872 | tf_op jit(solution)/shard_map/ppermute | solution.py:472
  27.8 0.0 collective-permute-done.8.twin_ref
  27.8 1.7 %shard_map.121 = (f32[224,768]{1,0:T(8,128)S(1)}, bf16[224,512]{1,0:T(8,128)(2,1)S(1)}, f32[224,256]{1,0:T(8,128)S(1)}) custom-call(f32[1,512]{1,0:T(1,128)S(1)} %get-tuple-element.20.gain_ref.key_gain_ref, bf16[224,512]{1,0:T(8,128)(2,1)S(1)} %get-tuple-element.30.own_ref.query_ref, bf16[224,512]{1,0:T(8,128)(2,1)S(1)} %collective-permute-done.8.twin_ref, ...), custom_call_target="tpu_custom_call" | custom-call | flops 2000000000 | bytes 4194304 | tf_op jit(solution)/shard_map/pallas_call | solution.py:25
  29.5 0.1 collective-permute-start.11
  29.6 0.0 copy-start
  29.6 0.0 copy-start.1
  29.6 0.5 %collective-permute-start.12 = (f32[224,256]{1,0:T(8,128)S(1)}, f32[224,256]{1,0:T(8,128)S(1)}, u32[]{:S(2)}, u32[]{:S(2)}) collective-permute-start(f32[224,256]{1,0:T(8,128)S(1)} %get-tuple-element.33), channel_id=1, source_target_pairs={{0,1},{1,0},{2,3},{3,2},{4,5},{5,4},{6,7},{7,6},{8,9},{9,8},{10,11... | collective-permute-start | bytes 688136 | tf_op jit(solution)/shard_map/ppermute | solution.py:472
  30.1 0.0 slice-done
  30.1 0.0 slice-done.1
  30.1 1.1 %shard_map.123.partial_ref = f32[160,256]{1,0:T(8,128)S(1)} custom-call(bf16[2,20,8,512]{3,2,1,0:T(8,128)(2,1)S(1)} %get-tuple-element.22.cache_ref, bf16[3,24,512]{2,1,0:T(8,128)(2,1)S(1)} %get-tuple-element.25.top_ref, bf16[3,24,512]{2,1,0:T(8,128)(2,1)S(1)} %get-tuple-element.26.bottom_ref, bf16[3,16,512]{2,1,0:T(8,128)(2,1)S(1)} %get-tuple-element.27.twin_ref, ...), custom_call_target="tpu_custom_call" | custom-call | flops 2000000000 | bytes 4194304 | tf_op jit(solution)/shard_map/pallas_call | solution.py:25
  31.2 0.0 collective-permute-done.7.block_ref
  31.2 0.2 collective-permute-start.13
  31.4 0.6 %shard_map.122.state_ref = f32[224,768]{1,0:T(8,128)S(1)} custom-call(f32[1,512]{1,0:T(1,128)S(1)} %get-tuple-element.20.gain_ref.key_gain_ref, bf16[224,512]{1,0:T(8,128)(2,1)S(1)} %get-tuple-element.30.own_ref.query_ref, bf16[160,512]{1,0:T(8,128)(2,1)S(1)} %collective-permute-done.7.block_ref, f32[224,768]{1,0:T(8,128)S(1)} %get-tuple-element.31.state_ref), custom_call_target="tpu_custom_call" | custom-call | flops 2000000000 | bytes 4194304 | tf_op jit(solution)/shard_map/pallas_call | solution.py:25
  32.0 0.7 %collective-permute-done.13.last_ref = bf16[160,512]{1,0:T(8,128)(2,1)S(1)} collective-permute-done((bf16[160,512]{1,0:T(8,128)(2,1)S(1)}, bf16[160,512]{1,0:T(8,128)(2,1)S(1)}, u32[]{:S(2)}, u32[]{:S(2)}) %collective-permute-start.13) | collective-permute-done | bytes 163872 | tf_op jit(solution)/shard_map/ppermute | solution.py:472
  32.7 0.0 collective-permute-done.11.other_ref
  32.7 0.0 collective-permute-done.12.scale_ref
  32.7 0.0 copy-done
  32.7 0.0 copy-done.1
  32.7 2.3 %shard_map.124 = (bf16[160,512]{1,0:T(8,128)(2,1)}, bf16[160,256]{1,0:T(8,128)(2,1)}) custom-call(f32[224,768]{1,0:T(8,128)S(1)} %shard_map.122.state_ref, bf16[224,512]{1,0:T(8,128)(2,1)S(1)} %collective-permute-done.11.other_ref, f32[224,256]{1,0:T(8,128)S(1)} %collective-permute-done.12.scale_ref, ...), custom_call_target="tpu_custom_call" | custom-call | flops 2000000000 | bytes 4194304 | tf_op jit(solution)/shard_map/pallas_call | solution.py:25
  (3 shorter events, 0.0 us)
Async XLA Ops:
  1.8 3.2 %collective-permute-start = (bf16[208,512]{1,0:T(8,128)(2,1)S(1)}, bf16[208,512]{1,0:T(8,128)(2,1)S(1)}, u32[]{:S(2)}, u32[]{:S(2)}) collective-permute-start(bf16[208,512]{1,0:T(8,128)(2,1)S(1)} %get-tuple-element.23), channel_id=1, source_target_pairs={{0,1},{1,0},{2,3},{3,2},{4,5},{5,4},{6,7},{7,6},{8,9},{9,8},{10,11... | collective-permute-start | bytes 638984 | tf_op jit(solution)/shard_map/ppermute | solution.py:472
  2.4 8.9 %copy-start.2 = (bf16[512,512]{1,0:T(8,128)(2,1)S(1)}, bf16[512,512]{1,0:T(8,128)(2,1)}, u32[]{:S(2)}) copy-start(bf16[512,512]{1,0:T(8,128)(2,1)} %wq_ref.1) | copy-start | bytes 1572868
  2.4 8.9 %copy-start.3 = (bf16[512,512]{1,0:T(8,128)(2,1)S(1)}, bf16[512,512]{1,0:T(8,128)(2,1)}, u32[]{:S(2)}) copy-start(bf16[512,512]{1,0:T(8,128)(2,1)} %wk_ref.1) | copy-start | bytes 1572868
  2.4 8.9 %copy-start.4 = (bf16[512,512]{1,0:T(8,128)(2,1)S(1)}, bf16[512,512]{1,0:T(8,128)(2,1)}, u32[]{:S(2)}) copy-start(bf16[512,512]{1,0:T(8,128)(2,1)} %wv_ref.1) | copy-start | bytes 1572868
  2.4 8.9 %copy-start.5 = (bf16[512,512]{1,0:T(8,128)(2,1)S(1)}, bf16[512,512]{1,0:T(8,128)(2,1)}, u32[]{:S(2)}) copy-start(bf16[512,512]{1,0:T(8,128)(2,1)} %wo_ref.1) | copy-start | bytes 1572868
  2.4 6.4 %collective-permute-start.1 = (bf16[208,512]{1,0:T(8,128)(2,1)S(1)}, bf16[208,512]{1,0:T(8,128)(2,1)S(1)}, u32[]{:S(2)}, u32[]{:S(2)}) collective-permute-start(bf16[208,512]{1,0:T(8,128)(2,1)S(1)} %get-tuple-element.24), channel_id=1, source_target_pairs={{4,8},{9,5},{8,12},{13,9},{12,14},{15,13},{14,10},{11,15},{10,6},{... | collective-permute-start | bytes 638984 | tf_op jit(solution)/shard_map/ppermute | solution.py:472
  5.1 6.0 %collective-permute-start.2 = (bf16[208,512]{1,0:T(8,128)(2,1)S(1)}, bf16[208,512]{1,0:T(8,128)(2,1)S(1)}, u32[]{:S(2)}, u32[]{:S(2)}) collective-permute-start(bf16[208,512]{1,0:T(8,128)(2,1)S(1)} %collective-permute-done.partner_ref), channel_id=1, source_target_pairs={{4,8},{9,5},{8,12},{13,9},{12,14},{15,13},{14,10},{11,15},{10,6},{... | collective-permute-start | bytes 638984 | tf_op jit(solution)/shard_map/ppermute | solution.py:472
  8.8 5.4 %collective-permute-start.5 = (bf16[160,512]{1,0:T(8,128)(2,1)S(1)}, bf16[160,512]{1,0:T(8,128)(2,1)S(1)}, u32[]{:S(2)}, u32[]{:S(2)}) collective-permute-start(bf16[160,512]{1,0:T(8,128)(2,1)S(1)} %shard_map.118.refs_1_), channel_id=1, source_target_pairs={{4,8},{9,5},{8,12},{13,9},{12,14},{15,13},{14,10},{11,15},{10,6},{... | collective-permute-start | bytes 491528 | tf_op jit(solution)/shard_map/ppermute | solution.py:472
  11.2 5.1 %collective-permute-start.3 = (bf16[160,512]{1,0:T(8,128)(2,1)S(1)}, bf16[160,512]{1,0:T(8,128)(2,1)S(1)}, u32[]{:S(2)}, u32[]{:S(2)}) collective-permute-start(bf16[160,512]{1,0:T(8,128)(2,1)S(1)} %shard_map.114.mine_ref), channel_id=1, source_target_pairs={{0,1},{1,0},{2,3},{3,2},{4,5},{5,4},{6,7},{7,6},{8,9},{9,8},{10,11... | collective-permute-start | bytes 491528 | tf_op jit(solution)/shard_map/ppermute | solution.py:472
  14.2 6.3 %collective-permute-start.6 = (bf16[160,512]{1,0:T(8,128)(2,1)S(1)}, bf16[160,512]{1,0:T(8,128)(2,1)S(1)}, u32[]{:S(2)}, u32[]{:S(2)}) collective-permute-start(bf16[160,512]{1,0:T(8,128)(2,1)S(1)} %collective-permute-done.5.refs_3_), channel_id=1, source_target_pairs={{4,8},{9,5},{8,12},{13,9},{12,14},{15,13},{14,10},{11,15},{10,6},{... | collective-permute-start | bytes 491528 | tf_op jit(solution)/shard_map/ppermute | solution.py:472
  16.4 2.3 %collective-permute-start.4 = (bf16[32,512]{1,0:T(8,128)(2,1)S(1)}, bf16[32,512]{1,0:T(8,128)(2,1)S(1)}, u32[]{:S(2)}, u32[]{:S(2)}) collective-permute-start(bf16[32,512]{1,0:T(8,128)(2,1)S(1)} %get-tuple-element.28), channel_id=1, source_target_pairs={{1,2},{2,1},{5,6},{6,5},{9,10},{10,9},{13,14},{14,13},{17,18},{18,... | collective-permute-start | bytes 98312 | tf_op jit(solution)/shard_map/ppermute | solution.py:472
  17.1 5.4 %collective-permute-start.9 = (bf16[160,512]{1,0:T(8,128)(2,1)S(1)}, bf16[160,512]{1,0:T(8,128)(2,1)S(1)}, u32[]{:S(2)}, u32[]{:S(2)}) collective-permute-start(bf16[160,512]{1,0:T(8,128)(2,1)S(1)} %shard_map.119.refs_2_), channel_id=1, source_target_pairs={{4,8},{9,5},{8,12},{13,9},{12,14},{15,13},{14,10},{11,15},{10,6},{... | collective-permute-start | bytes 491528 | tf_op jit(solution)/shard_map/ppermute | solution.py:472
  18.8 11.3 %slice-start = ((s8[7077888]{0:T(1024)(128)(4,1)}), s8[4194304]{0:T(1024)(128)(4,1)S(1)}, s32[]{:S(2)}) async-start(s8[7077888]{0:T(1024)(128)(4,1)} %bitcast.11), calls=%async_computation | async-start | bytes 8388608
  19.1 11.0 %slice-start.1 = ((s8[7077888]{0:T(1024)(128)(4,1)}), s8[2883584]{0:T(1024)(128)(4,1)S(1)}, s32[]{:S(2)}) async-start(s8[7077888]{0:T(1024)(128)(4,1)} %bitcast.11), calls=%async_computation.1 | async-start | bytes 5767168
  19.1 8.7 %collective-permute-start.8 = (bf16[224,512]{1,0:T(8,128)(2,1)S(1)}, bf16[224,512]{1,0:T(8,128)(2,1)S(1)}, u32[]{:S(2)}, u32[]{:S(2)}) collective-permute-start(bf16[224,512]{1,0:T(8,128)(2,1)S(1)} %get-tuple-element.30.own_ref.query_ref), channel_id=1, source_target_pairs={{0,1},{1,0},{2,3},{3,2},{4,5},{5,4},{6,7},{7,6},{8,9},{9,8},{10,11... | collective-permute-start | bytes 688136 | tf_op jit(solution)/shard_map/ppermute | solution.py:472
  20.5 10.7 %collective-permute-start.7 = (bf16[160,512]{1,0:T(8,128)(2,1)S(1)}, bf16[160,512]{1,0:T(8,128)(2,1)S(1)}, u32[]{:S(2)}, u32[]{:S(2)}) collective-permute-start(bf16[160,512]{1,0:T(8,128)(2,1)S(1)} %collective-permute-done.6.refs_1_), channel_id=1, source_target_pairs={{4,8},{9,5},{8,12},{13,9},{12,14},{15,13},{14,10},{11,15},{10,6},{... | collective-permute-start | bytes 491528 | tf_op jit(solution)/shard_map/ppermute | solution.py:472
  22.5 5.3 %collective-permute-start.10 = (bf16[160,512]{1,0:T(8,128)(2,1)S(1)}, bf16[160,512]{1,0:T(8,128)(2,1)S(1)}, u32[]{:S(2)}, u32[]{:S(2)}) collective-permute-start(bf16[160,512]{1,0:T(8,128)(2,1)S(1)} %collective-permute-done.9.refs_4_), channel_id=1, source_target_pairs={{4,8},{9,5},{8,12},{13,9},{12,14},{15,13},{14,10},{11,15},{10,6},{... | collective-permute-start | bytes 491528 | tf_op jit(solution)/shard_map/ppermute | solution.py:472
  29.5 3.2 %collective-permute-start.11 = (bf16[224,512]{1,0:T(8,128)(2,1)S(1)}, bf16[224,512]{1,0:T(8,128)(2,1)S(1)}, u32[]{:S(2)}, u32[]{:S(2)}) collective-permute-start(bf16[224,512]{1,0:T(8,128)(2,1)S(1)} %get-tuple-element.32), channel_id=1, source_target_pairs={{0,1},{1,0},{2,3},{3,2},{4,5},{5,4},{6,7},{7,6},{8,9},{9,8},{10,11... | collective-permute-start | bytes 688136 | tf_op jit(solution)/shard_map/ppermute | solution.py:472
  29.6 3.1 %copy-start = (f32[512]{0:T(512)S(1)}, f32[512]{0:T(512)}, u32[]{:S(2)}) copy-start(f32[512]{0:T(512)} %param.16) | copy-start | bytes 6148
  29.6 3.1 %copy-start.1 = (f32[256]{0:T(256)S(1)}, f32[256]{0:T(256)}, u32[]{:S(2)}) copy-start(f32[256]{0:T(256)} %param.19) | copy-start | bytes 3076
  29.6 3.1 %collective-permute-start.12 = (f32[224,256]{1,0:T(8,128)S(1)}, f32[224,256]{1,0:T(8,128)S(1)}, u32[]{:S(2)}, u32[]{:S(2)}) collective-permute-start(f32[224,256]{1,0:T(8,128)S(1)} %get-tuple-element.33), channel_id=1, source_target_pairs={{0,1},{1,0},{2,3},{3,2},{4,5},{5,4},{6,7},{7,6},{8,9},{9,8},{10,11... | collective-permute-start | bytes 688136 | tf_op jit(solution)/shard_map/ppermute | solution.py:472
  31.2 1.5 %collective-permute-start.13 = (bf16[160,512]{1,0:T(8,128)(2,1)S(1)}, bf16[160,512]{1,0:T(8,128)(2,1)S(1)}, u32[]{:S(2)}, u32[]{:S(2)}) collective-permute-start(bf16[160,512]{1,0:T(8,128)(2,1)S(1)} %collective-permute-done.7.block_ref), channel_id=1, source_target_pairs={{0,1},{1,0},{2,3},{3,2},{4,5},{5,4},{6,7},{7,6},{8,9},{9,8},{10,11... | collective-permute-start | bytes 491528 | tf_op jit(solution)/shard_map/ppermute | solution.py:472
